TPU v7x, 1024 devices: a whole 8x8x8 slice. The times are simulated.
1024 devices in a mesh: lat: 4 (over y_hi), lon: 256 (over y_lo, x, z, core).
Axes of the slice: x: 8, y: 8 (y_hi: 4, y_lo: 2; y = y_hi * 2 + y_lo), z: 8, core: 2. Of those that a mesh axis runs over, the one named last changes fastest.
Arguments:
- fields: bfloat16 [64, 4096, 128], P('lat', 'lon'), may hold values from -6 to 6
- weight_one: bfloat16 [7, 128, 128], replicated, may hold values from -0.1875 to 0.1875
- weight_two: bfloat16 [7, 128, 128], replicated, may hold values from -0.1875 to 0.1875
- basis_raw: bfloat16 [7, 64, 3, 9], replicated, may hold values from -1.5 to 1.5
- widths: int32 [64], replicated, may hold values from 1 to 4, as said below
- cotangent: bfloat16 [64, 4096, 128], P('lat', 'lon'), may hold values from -6 to 6
Outputs:
- output: bfloat16 [64, 4096, 128], P('lat', 'lon')
- dfields: bfloat16 [64, 4096, 128], P('lat', 'lon')
- grad_one: float32 [7, 128, 128], replicated
- grad_two: float32 [7, 128, 128], replicated
Inputs may be any that keep to these rules, and one draw needn't show every extreme that they name: widths is 4 on the first and the last row of the grid.
All inputs are finite; a program needn't handle non-finite values.
Results may differ from a plain program's by a relative error of at most 0.0076.
Values may be sent and summed in bfloat16 or wider, within the bound.
A program may use at most 32 MiB of HBM per device.

v0:
```python
import math

import jax
import jax.numpy as jnp
from jax import lax
from jax.sharding import PartitionSpec as P


def shifted(block, axis, distance):
    devices = range(lax.axis_size(axis))
    route = [((i - distance) % len(devices), i) for i in devices]
    return lax.ppermute(block, axis, route)


def with_halo(block, sides, width, periodic):
    for axis, dim in sides:
        count = lax.axis_size(axis)
        forward = [(i, i + 1) for i in range(count - 1)]
        if periodic:
            forward.append((count - 1, 0))
        backward = [(target, source) for source, target in forward]
        low = lax.ppermute(
            lax.slice_in_dim(block, block.shape[dim] - width, None, axis=dim), axis, forward
        )
        high = lax.ppermute(lax.slice_in_dim(block, 0, width, axis=dim), axis, backward)
        block = jnp.concatenate([low, block, high], axis=dim)
    return block


def gelu_back(pre, upstream):
    return jax.vjp(jax.nn.gelu, pre)[1](upstream)[0]


def padded_basis(basis_raw, widths):
    tap_count = basis_raw.shape[3]
    reach = (tap_count - 1) // 2
    distance = jnp.abs(jnp.arange(tap_count, dtype=jnp.int32) - reach)
    inside = (distance[None, :] <= widths[:, None]).astype(jnp.bfloat16)
    masked = basis_raw * inside[None, :, None, :]
    top_rows = masked[:, 0:1, ::-1, :]
    bottom = masked[:, -1:, ::-1, :]
    zero_row = jnp.zeros_like(top_rows)
    return jnp.concatenate([zero_row, top_rows, masked, bottom, zero_row], axis=1)


def selector(out_len, in_len, tap_count, flipped):
    lon_out = jnp.arange(out_len, dtype=jnp.int32)[None, :, None]
    lon_in = jnp.arange(in_len, dtype=jnp.int32)[None, None, :]
    offset = jnp.arange(tap_count, dtype=jnp.int32)[:, None, None]
    target = lon_out + (tap_count - 1) - offset if flipped else lon_out + offset
    return (lon_in == target).astype(jnp.bfloat16)


def spread_local(extended, basis_rows):
    row_count = basis_rows.shape[1]
    tap_count = basis_rows.shape[3]
    in_len = extended.shape[1]
    out_len = in_len - (tap_count - 1)
    picker = selector(out_len, in_len, tap_count, False)
    summed = None
    for row_tap in range(3):
        band_rows = jnp.einsum(
            "kit,tlm->kilm",
            basis_rows[:, :, row_tap, :],
            picker,
            preferred_element_type=jnp.float32,
        ).astype(jnp.bfloat16)
        partial_rows = jnp.einsum(
            "kilm,imc->ilkc",
            band_rows,
            extended[row_tap : row_tap + row_count],
            preferred_element_type=jnp.float32,
        )
        summed = partial_rows if summed is None else summed + partial_rows
    return summed.astype(jnp.bfloat16)


def gather_back(extended, source_basis):
    row_count = extended.shape[0] - 2
    tap_count = source_basis.shape[3]
    in_len = extended.shape[1]
    out_len = in_len - (tap_count - 1)
    picker = selector(out_len, in_len, tap_count, True)
    summed = None
    for row_tap in range(3):
        first_tap = 2 - row_tap
        weights_rows = source_basis[:, first_tap : first_tap + row_count, row_tap, :]
        band_rows = jnp.einsum(
            "kjt,tlm->kjlm", weights_rows, picker, preferred_element_type=jnp.float32
        ).astype(jnp.bfloat16)
        partial_rows = jnp.einsum(
            "kjlm,jmkc->jlc",
            band_rows,
            extended[first_tap : first_tap + row_count],
            preferred_element_type=jnp.float32,
        )
        summed = partial_rows if summed is None else summed + partial_rows
    return summed


def mix_forward(spread_vals, weight):
    return jnp.einsum("ilkc,kco->ilo", spread_vals, weight, preferred_element_type=jnp.float32)


def mix_back(dconv, weight):
    return jnp.einsum("ilo,kco->ilkc", dconv, weight, preferred_element_type=jnp.float32).astype(
        jnp.bfloat16
    )


def weight_terms(spread_vals, dconv):
    return jnp.einsum("ilkc,ilo->kco", spread_vals, dconv, preferred_element_type=jnp.float32)


def mirror_fix(heightened, depth):
    row_count = heightened.shape[0] - 2 * depth
    top_rows = jnp.flip(heightened[depth : 2 * depth], 0)
    bottom = jnp.flip(heightened[row_count : row_count + depth], 0)
    mirrored = shifted(jnp.concatenate([top_rows, bottom], 0), "lon", lax.axis_size("lon") // 2)
    band_index = lax.axis_index("lat")
    new_top = jnp.where(band_index == 0, mirrored[:depth], heightened[:depth])
    new_bottom = jnp.where(
        band_index == lax.axis_size("lat") - 1, mirrored[depth:], heightened[row_count + depth :]
    )
    return jnp.concatenate([new_top, heightened[depth : row_count + depth], new_bottom], 0)


def extend_each(field, reach):
    widened = with_halo(field, (("lon", 1),), reach, True)
    heightened = with_halo(widened, (("lat", 0),), 1, False)
    return mirror_fix(heightened, 1)


def body(fields, weight_one, weight_two, basis_raw, widths, cotangent):
    lat_count = fields.shape[0]
    lon_count = fields.shape[1]
    reach = (basis_raw.shape[3] - 1) // 2
    basis = padded_basis(basis_raw, widths)
    first_row = lax.axis_index("lat") * lat_count

    def output_rows(row_count):
        return lax.dynamic_slice_in_dim(basis, first_row + 2, row_count, 1)

    def source_rows(row_count):
        return lax.dynamic_slice_in_dim(basis, first_row + 1, row_count + 2, 1)

    upstream = cotangent.astype(jnp.float32)
    ext_fields = extend_each(fields, reach)
    u_one = spread_local(ext_fields, output_rows(lat_count))
    pre_one = mix_forward(u_one, weight_one)
    hidden = (fields.astype(jnp.float32) + jax.nn.gelu(pre_one)).astype(jnp.bfloat16)
    ext_hidden = extend_each(hidden, reach)
    u_two = spread_local(ext_hidden, output_rows(lat_count))
    pre_two = mix_forward(u_two, weight_two)
    output = (hidden.astype(jnp.float32) + jax.nn.gelu(pre_two)).astype(jnp.bfloat16)
    dconv_two = gelu_back(pre_two, upstream).astype(jnp.bfloat16)
    grad_two = weight_terms(u_two, dconv_two)
    ext_two = extend_each(dconv_two, reach)
    du_two = mix_back(ext_two, weight_two)
    dhidden = upstream + gather_back(du_two, source_rows(lat_count))
    dconv_one = gelu_back(pre_one, dhidden).astype(jnp.bfloat16)
    ext_one = extend_each(dconv_one, reach)
    grad_one = weight_terms(u_one, dconv_one)
    du_one = mix_back(ext_one, weight_one)
    dfields = (dhidden + gather_back(du_one, source_rows(lat_count))).astype(jnp.bfloat16)
    summed_one, summed_two = lax.psum((grad_one, grad_two), ("lat", "lon"))
    scale = 1.0 / math.sqrt(lat_count * lax.axis_size("lat") * lon_count * lax.axis_size("lon"))
    return (output, dfields, summed_one * scale, summed_two * scale)


def solution(mesh):
    placed = (P("lat", "lon", None), P(), P(), P(), P(), P("lat", "lon", None))
    return jax.shard_map(
        body,
        mesh=mesh,
        in_specs=placed,
        out_specs=(P("lat", "lon", None), P("lat", "lon", None), P(), P()),
        check_vma=False,
    )
```

profile of v0, /device:TPU:1, one launch (start us, length us, event | category | flops | bytes accessed | tf_op | source)
XLA Modules:
  0.0 422.0 jit_solution(13370712254847101509)
XLA Ops:
  7.2 0.8 fusion.115
  8.1 6.3 %collective-permute-start = (bf16[16,4,128]{2,1,0:T(4,128)(2,1)S(1)}, bf16[16,4,128]{2,1,0:T(4,128)(2,1)S(1)}, u32[]{:S(2)}, u32[]{:S(2)}) collective-permute-start(bf16[16,4,128]{2,1,0:T(4,128)(2,1)S(1)} %get-tuple-element.22), channel_id=1, source_target_pairs={{0,1},{1,2},{2,3},{3,4},{4,5},{5,6},{6,7},{7,8},{8,9},{9,10},{10,1... | collective-permute-start | bytes 49160 | tf_op jit(solution)/shard_map/ppermute | solution.py:22
  14.4 11.7 %collective-permute-start.1 = (bf16[16,4,128]{2,1,0:T(4,128)(2,1)S(1)}, bf16[16,4,128]{2,1,0:T(4,128)(2,1)S(1)}, u32[]{:S(2)}, u32[]{:S(2)}) collective-permute-start(bf16[16,4,128]{2,1,0:T(4,128)(2,1)S(1)} %get-tuple-element.23), channel_id=1, source_target_pairs={{1,0},{2,1},{3,2},{4,3},{5,4},{6,5},{7,6},{8,7},{9,8},{10,9},{11,1... | collective-permute-start | bytes 49160 | tf_op jit(solution)/shard_map/ppermute | solution.py:25
  26.1 0.7 compare_convert_fusion
  26.9 0.8 broadcast_multiply_fusion.2
  27.8 0.2 concatenate.50
  28.1 0.1 copy.69
  28.2 0.1 copy.68
  28.4 0.3 convolution_convert_fusion.6
  28.7 0.3 convolution_convert_fusion.7
  29.0 0.1 copy.70
  29.2 0.3 convolution_convert_fusion.5
  29.8 1.3 collective-permute-start.3
  31.1 1.3 collective-permute-start.4
  32.4 1.9 collective-permute-start.2
  34.3 0.3 fusion.27
  34.6 1.8 collective-permute-done.4
  36.4 0.5 collective-permute-done.2
  36.9 0.3 convolution_add_fusion.3
  37.1 0.3 fusion.3
  37.4 0.6 copy-done.2
  38.1 0.3 add_convert_fusion.1
  38.4 1.9 collective-permute-start.5
  40.3 12.1 %collective-permute-start.6 = (bf16[16,4,128]{2,1,0:T(4,128)(2,1)S(1)}, bf16[16,4,128]{2,1,0:T(4,128)(2,1)S(1)}, u32[]{:S(2)}, u32[]{:S(2)}) collective-permute-start(bf16[16,4,128]{2,1,0:T(4,128)(2,1)S(1)} %get-tuple-element.21), channel_id=1, source_target_pairs={{1,0},{2,1},{3,2},{4,3},{5,4},{6,5},{7,6},{8,7},{9,8},{10,9},{11,1... | collective-permute-start | bytes 49160 | tf_op jit(solution)/shard_map/ppermute | solution.py:25
  52.5 0.3 convolution_convert_fusion.3
  52.8 0.1 copy.74
  52.9 0.3 collective-permute-done.6
  53.3 5.5 %collective-permute-start.8 = (bf16[1,24,128]{2,1,0:T(8,128)(2,1)S(1)}, bf16[1,24,128]{2,1,0:T(8,128)(2,1)S(1)}, u32[]{:S(2)}, u32[]{:S(2)}) collective-permute-start(bf16[1,24,128]{2,1,0:T(8,128)(2,1)S(1)} %get-tuple-element.13), channel_id=1, source_target_pairs={{0,256},{256,512},{512,768},{1,257},{257,513},{513,769},{2,258},{2... | collective-permute-start | bytes 18440 | tf_op jit(solution)/shard_map/ppermute | solution.py:22
  58.9 1.3 collective-permute-start.9
  60.2 2.9 collective-permute-start.7
  63.0 0.3 fusion.25
  63.3 2.2 collective-permute-done.9
  65.5 0.3 convolution_add_fusion.1
  65.8 0.3 fusion.2
  66.1 0.5 copy-done.3
  66.6 1.0 fusion.48
  67.7 1.9 collective-permute-start.10
  69.6 9.6 %collective-permute-start.11 = (bf16[16,4,128]{2,1,0:T(4,128)(2,1)S(1)}, bf16[16,4,128]{2,1,0:T(4,128)(2,1)S(1)}, u32[]{:S(2)}, u32[]{:S(2)}) collective-permute-start(bf16[16,4,128]{2,1,0:T(4,128)(2,1)S(1)} %get-tuple-element.19), channel_id=1, source_target_pairs={{1,0},{2,1},{3,2},{4,3},{5,4},{6,5},{7,6},{8,7},{9,8},{10,9},{11,1... | collective-permute-start | bytes 49160 | tf_op jit(solution)/shard_map/ppermute | solution.py:25
  79.2 0.3 convolution_convert_fusion.2
  79.5 0.1 copy.72
  79.7 0.4 collective-permute-done.11
  80.0 5.7 %collective-permute-start.13 = (bf16[1,24,128]{2,1,0:T(8,128)(2,1)S(1)}, bf16[1,24,128]{2,1,0:T(8,128)(2,1)S(1)}, u32[]{:S(2)}, u32[]{:S(2)}) collective-permute-start(bf16[1,24,128]{2,1,0:T(8,128)(2,1)S(1)} %get-tuple-element.10), channel_id=1, source_target_pairs={{0,256},{256,512},{512,768},{1,257},{257,513},{513,769},{2,258},{2... | collective-permute-start | bytes 18440 | tf_op jit(solution)/shard_map/ppermute | solution.py:22
  85.8 1.3 collective-permute-start.14
  87.1 2.9 collective-permute-start.12
  90.0 0.3 convolution_convert_fusion.4
  90.3 2.1 collective-permute-done.14
  92.5 0.4 convolution_convert_fusion.1
  92.9 0.5 convolution_bitcast_fusion.6
  93.4 0.5 convolution_bitcast_fusion.5
  93.9 0.5 fusion.41
  94.4 1.9 collective-permute-start.15
  96.4 9.6 %collective-permute-start.16 = (bf16[16,4,128]{2,1,0:T(4,128)(2,1)S(1)}, bf16[16,4,128]{2,1,0:T(4,128)(2,1)S(1)}, u32[]{:S(2)}, u32[]{:S(2)}) collective-permute-start(bf16[16,4,128]{2,1,0:T(4,128)(2,1)S(1)} %get-tuple-element.17), channel_id=1, source_target_pairs={{1,0},{2,1},{3,2},{4,3},{5,4},{6,5},{7,6},{8,7},{9,8},{10,9},{11,1... | collective-permute-start | bytes 49160 | tf_op jit(solution)/shard_map/ppermute | solution.py:25
  106.0 1.1 convolution_bitcast_fusion
  107.1 5.7 %collective-permute-start.18 = (bf16[1,24,128]{2,1,0:T(8,128)(2,1)S(1)}, bf16[1,24,128]{2,1,0:T(8,128)(2,1)S(1)}, u32[]{:S(2)}, u32[]{:S(2)}) collective-permute-start(bf16[1,24,128]{2,1,0:T(8,128)(2,1)S(1)} %get-tuple-element.8), channel_id=1, source_target_pairs={{0,256},{256,512},{512,768},{1,257},{257,513},{513,769},{2,258},{2... | collective-permute-start | bytes 18440 | tf_op jit(solution)/shard_map/ppermute | solution.py:22
  112.9 1.3 collective-permute-start.19
  114.2 2.9 collective-permute-start.17
  117.0 1.1 convolution_bitcast_fusion.1
  118.2 1.3 collective-permute-done.19
  119.5 0.4 convolution_convert_fusion
  120.0 0.5 convolution_bitcast_fusion.3
  120.5 0.5 convolution_bitcast_fusion.2
  121.0 1.1 fusion.10
  122.1 290.9 %all-reduce.3.cloned.1.call-done = (f32[7,128,128]{2,1,0:T(8,128)}, f32[7,128,128]{2,1,0:T(8,128)}) async-done(((f32[7,128,128]{2,1,0:T(8,128)}, f32[7,128,128]{2,1,0:T(8,128)}), (f32[7,128,128]{2,1,0:T(8,128)}, f32[7,128,128]{2,1,0:T(8,128)})) %all-reduce.3.cloned.1.call-update) | async-done | bytes 917520 | tf_op jit(solution)/shard_map/psum | solution.py:166
  413.0 2.1 broadcast_multiply_fusion
  (48 shorter events, 0.8 us)
Async XLA Ops:
  7.2 58.9 %copy-start = (bf16[7,128,128]{2,1,0:T(8,128)(2,1)S(1)}, bf16[7,128,128]{2,1,0:T(8,128)(2,1)}, u32[]{:S(2)}) copy-start(bf16[7,128,128]{2,1,0:T(8,128)(2,1)} %param.8) | copy-start | bytes 688132
  7.2 405.8 %all-reduce.3.cloned.1.call-start = ((), (), s32[]{:S(2)}) async-start(), calls=%async_computation | async-start | bytes 1835008 | tf_op jit(solution)/shard_map/psum | solution.py:166
  8.1 21.6 %collective-permute-start = (bf16[16,4,128]{2,1,0:T(4,128)(2,1)S(1)}, bf16[16,4,128]{2,1,0:T(4,128)(2,1)S(1)}, u32[]{:S(2)}, u32[]{:S(2)}) collective-permute-start(bf16[16,4,128]{2,1,0:T(4,128)(2,1)S(1)} %get-tuple-element.22), channel_id=1, source_target_pairs={{0,1},{1,2},{2,3},{3,4},{4,5},{5,6},{6,7},{7,8},{8,9},{9,10},{10,1... | collective-permute-start | bytes 49160 | tf_op jit(solution)/shard_map/ppermute | solution.py:22
  14.4 15.3 %collective-permute-start.1 = (bf16[16,4,128]{2,1,0:T(4,128)(2,1)S(1)}, bf16[16,4,128]{2,1,0:T(4,128)(2,1)S(1)}, u32[]{:S(2)}, u32[]{:S(2)}) collective-permute-start(bf16[16,4,128]{2,1,0:T(4,128)(2,1)S(1)} %get-tuple-element.23), channel_id=1, source_target_pairs={{1,0},{2,1},{3,2},{4,3},{5,4},{6,5},{7,6},{8,7},{9,8},{10,9},{11,1... | collective-permute-start | bytes 49160 | tf_op jit(solution)/shard_map/ppermute | solution.py:25
  28.0 1.7 copy-start.1
  29.8 4.8 %collective-permute-start.3 = (bf16[1,24,128]{2,1,0:T(8,128)(2,1)S(1)}, bf16[1,24,128]{2,1,0:T(8,128)(2,1)S(1)}, u32[]{:S(2)}, u32[]{:S(2)}) collective-permute-start(bf16[1,24,128]{2,1,0:T(8,128)(2,1)S(1)} %get-tuple-element.15), channel_id=1, source_target_pairs={{0,256},{256,512},{512,768},{1,257},{257,513},{513,769},{2,258},{2... | collective-permute-start | bytes 18440 | tf_op jit(solution)/shard_map/ppermute | solution.py:22
  31.1 5.3 %collective-permute-start.4 = (bf16[1,24,128]{2,1,0:T(8,128)(2,1)S(1)}, bf16[1,24,128]{2,1,0:T(8,128)(2,1)S(1)}, u32[]{:S(2)}, u32[]{:S(2)}) collective-permute-start(bf16[1,24,128]{2,1,0:T(8,128)(2,1)S(1)} %get-tuple-element.14), channel_id=1, source_target_pairs={{256,0},{512,256},{768,512},{257,1},{513,257},{769,513},{258,2},{5... | collective-permute-start | bytes 18440 | tf_op jit(solution)/shard_map/ppermute | solution.py:25
  32.4 4.4 %collective-permute-start.2 = (bf16[2,24,128]{2,1,0:T(8,128)(2,1)S(1)}, bf16[2,24,128]{2,1,0:T(8,128)(2,1)S(1)}, u32[]{:S(2)}, u32[]{:S(2)}) collective-permute-start(bf16[2,24,128]{2,1,0:T(8,128)(2,1)S(1)} %pad_maximum_fusion.22), channel_id=1, source_target_pairs={{128,0},{129,1},{130,2},{131,3},{132,4},{133,5},{134,6},{135,7},{1... | collective-permute-start | bytes 36872 | tf_op jit(solution)/shard_map/ppermute | solution.py:12
  37.1 0.9 copy-start.2
  38.4 14.5 %collective-permute-start.5 = (bf16[16,4,128]{2,1,0:T(4,128)(2,1)S(1)}, bf16[16,4,128]{2,1,0:T(4,128)(2,1)S(1)}, u32[]{:S(2)}, u32[]{:S(2)}) collective-permute-start(bf16[16,4,128]{2,1,0:T(4,128)(2,1)S(1)} %get-tuple-element.20), channel_id=1, source_target_pairs={{0,1},{1,2},{2,3},{3,4},{4,5},{5,6},{6,7},{7,8},{8,9},{9,10},{10,1... | collective-permute-start | bytes 49160 | tf_op jit(solution)/shard_map/ppermute | solution.py:22
  40.3 12.9 %collective-permute-start.6 = (bf16[16,4,128]{2,1,0:T(4,128)(2,1)S(1)}, bf16[16,4,128]{2,1,0:T(4,128)(2,1)S(1)}, u32[]{:S(2)}, u32[]{:S(2)}) collective-permute-start(bf16[16,4,128]{2,1,0:T(4,128)(2,1)S(1)} %get-tuple-element.21), channel_id=1, source_target_pairs={{1,0},{2,1},{3,2},{4,3},{5,4},{6,5},{7,6},{8,7},{9,8},{10,9},{11,1... | collective-permute-start | bytes 49160 | tf_op jit(solution)/shard_map/ppermute | solution.py:25
  53.3 10.0 %collective-permute-start.8 = (bf16[1,24,128]{2,1,0:T(8,128)(2,1)S(1)}, bf16[1,24,128]{2,1,0:T(8,128)(2,1)S(1)}, u32[]{:S(2)}, u32[]{:S(2)}) collective-permute-start(bf16[1,24,128]{2,1,0:T(8,128)(2,1)S(1)} %get-tuple-element.13), channel_id=1, source_target_pairs={{0,256},{256,512},{512,768},{1,257},{257,513},{513,769},{2,258},{2... | collective-permute-start | bytes 18440 | tf_op jit(solution)/shard_map/ppermute | solution.py:22
  58.9 6.7 %collective-permute-start.9 = (bf16[1,24,128]{2,1,0:T(8,128)(2,1)S(1)}, bf16[1,24,128]{2,1,0:T(8,128)(2,1)S(1)}, u32[]{:S(2)}, u32[]{:S(2)}) collective-permute-start(bf16[1,24,128]{2,1,0:T(8,128)(2,1)S(1)} %get-tuple-element.12), channel_id=1, source_target_pairs={{256,0},{512,256},{768,512},{257,1},{513,257},{769,513},{258,2},{5... | collective-permute-start | bytes 18440 | tf_op jit(solution)/shard_map/ppermute | solution.py:25
  60.2 5.4 %collective-permute-start.7 = (bf16[2,24,128]{2,1,0:T(8,128)(2,1)S(1)}, bf16[2,24,128]{2,1,0:T(8,128)(2,1)S(1)}, u32[]{:S(2)}, u32[]{:S(2)}) collective-permute-start(bf16[2,24,128]{2,1,0:T(8,128)(2,1)S(1)} %pad_maximum_fusion.23), channel_id=1, source_target_pairs={{128,0},{129,1},{130,2},{131,3},{132,4},{133,5},{134,6},{135,7},{1... | collective-permute-start | bytes 36872 | tf_op jit(solution)/shard_map/ppermute | solution.py:12
  65.8 0.8 copy-start.3
  67.7 12.0 %collective-permute-start.10 = (bf16[16,4,128]{2,1,0:T(4,128)(2,1)S(1)}, bf16[16,4,128]{2,1,0:T(4,128)(2,1)S(1)}, u32[]{:S(2)}, u32[]{:S(2)}) collective-permute-start(bf16[16,4,128]{2,1,0:T(4,128)(2,1)S(1)} %get-tuple-element.18), channel_id=1, source_target_pairs={{0,1},{1,2},{2,3},{3,4},{4,5},{5,6},{6,7},{7,8},{8,9},{9,10},{10,1... | collective-permute-start | bytes 49160 | tf_op jit(solution)/shard_map/ppermute | solution.py:22
  69.6 10.4 %collective-permute-start.11 = (bf16[16,4,128]{2,1,0:T(4,128)(2,1)S(1)}, bf16[16,4,128]{2,1,0:T(4,128)(2,1)S(1)}, u32[]{:S(2)}, u32[]{:S(2)}) collective-permute-start(bf16[16,4,128]{2,1,0:T(4,128)(2,1)S(1)} %get-tuple-element.19), channel_id=1, source_target_pairs={{1,0},{2,1},{3,2},{4,3},{5,4},{6,5},{7,6},{8,7},{9,8},{10,9},{11,1... | collective-permute-start | bytes 49160 | tf_op jit(solution)/shard_map/ppermute | solution.py:25
  80.0 10.3 %collective-permute-start.13 = (bf16[1,24,128]{2,1,0:T(8,128)(2,1)S(1)}, bf16[1,24,128]{2,1,0:T(8,128)(2,1)S(1)}, u32[]{:S(2)}, u32[]{:S(2)}) collective-permute-start(bf16[1,24,128]{2,1,0:T(8,128)(2,1)S(1)} %get-tuple-element.10), channel_id=1, source_target_pairs={{0,256},{256,512},{512,768},{1,257},{257,513},{513,769},{2,258},{2... | collective-permute-start | bytes 18440 | tf_op jit(solution)/shard_map/ppermute | solution.py:22
  85.8 6.6 %collective-permute-start.14 = (bf16[1,24,128]{2,1,0:T(8,128)(2,1)S(1)}, bf16[1,24,128]{2,1,0:T(8,128)(2,1)S(1)}, u32[]{:S(2)}, u32[]{:S(2)}) collective-permute-start(bf16[1,24,128]{2,1,0:T(8,128)(2,1)S(1)} %get-tuple-element.11), channel_id=1, source_target_pairs={{256,0},{512,256},{768,512},{257,1},{513,257},{769,513},{258,2},{5... | collective-permute-start | bytes 18440 | tf_op jit(solution)/shard_map/ppermute | solution.py:25
  87.1 5.3 %collective-permute-start.12 = (bf16[2,24,128]{2,1,0:T(8,128)(2,1)S(1)}, bf16[2,24,128]{2,1,0:T(8,128)(2,1)S(1)}, u32[]{:S(2)}, u32[]{:S(2)}) collective-permute-start(bf16[2,24,128]{2,1,0:T(8,128)(2,1)S(1)} %pad_maximum_fusion.24), channel_id=1, source_target_pairs={{128,0},{129,1},{130,2},{131,3},{132,4},{133,5},{134,6},{135,7},{1... | collective-permute-start | bytes 36872 | tf_op jit(solution)/shard_map/ppermute | solution.py:12
  94.4 12.7 %collective-permute-start.15 = (bf16[16,4,128]{2,1,0:T(4,128)(2,1)S(1)}, bf16[16,4,128]{2,1,0:T(4,128)(2,1)S(1)}, u32[]{:S(2)}, u32[]{:S(2)}) collective-permute-start(bf16[16,4,128]{2,1,0:T(4,128)(2,1)S(1)} %get-tuple-element.16), channel_id=1, source_target_pairs={{0,1},{1,2},{2,3},{3,4},{4,5},{5,6},{6,7},{7,8},{8,9},{9,10},{10,1... | collective-permute-start | bytes 49160 | tf_op jit(solution)/shard_map/ppermute | solution.py:22
  96.4 10.7 %collective-permute-start.16 = (bf16[16,4,128]{2,1,0:T(4,128)(2,1)S(1)}, bf16[16,4,128]{2,1,0:T(4,128)(2,1)S(1)}, u32[]{:S(2)}, u32[]{:S(2)}) collective-permute-start(bf16[16,4,128]{2,1,0:T(4,128)(2,1)S(1)} %get-tuple-element.17), channel_id=1, source_target_pairs={{1,0},{2,1},{3,2},{4,3},{5,4},{6,5},{7,6},{8,7},{9,8},{10,9},{11,1... | collective-permute-start | bytes 49160 | tf_op jit(solution)/shard_map/ppermute | solution.py:25
  107.1 11.1 %collective-permute-start.18 = (bf16[1,24,128]{2,1,0:T(8,128)(2,1)S(1)}, bf16[1,24,128]{2,1,0:T(8,128)(2,1)S(1)}, u32[]{:S(2)}, u32[]{:S(2)}) collective-permute-start(bf16[1,24,128]{2,1,0:T(8,128)(2,1)S(1)} %get-tuple-element.8), channel_id=1, source_target_pairs={{0,256},{256,512},{512,768},{1,257},{257,513},{513,769},{2,258},{2... | collective-permute-start | bytes 18440 | tf_op jit(solution)/shard_map/ppermute | solution.py:22
  112.9 6.6 %collective-permute-start.19 = (bf16[1,24,128]{2,1,0:T(8,128)(2,1)S(1)}, bf16[1,24,128]{2,1,0:T(8,128)(2,1)S(1)}, u32[]{:S(2)}, u32[]{:S(2)}) collective-permute-start(bf16[1,24,128]{2,1,0:T(8,128)(2,1)S(1)} %get-tuple-element.9), channel_id=1, source_target_pairs={{256,0},{512,256},{768,512},{257,1},{513,257},{769,513},{258,2},{5... | collective-permute-start | bytes 18440 | tf_op jit(solution)/shard_map/ppermute | solution.py:25
  114.2 5.4 %collective-permute-start.17 = (bf16[2,24,128]{2,1,0:T(8,128)(2,1)S(1)}, bf16[2,24,128]{2,1,0:T(8,128)(2,1)S(1)}, u32[]{:S(2)}, u32[]{:S(2)}) collective-permute-start(bf16[2,24,128]{2,1,0:T(8,128)(2,1)S(1)} %pad_maximum_fusion.25), channel_id=1, source_target_pairs={{128,0},{129,1},{130,2},{131,3},{132,4},{133,5},{134,6},{135,7},{1... | collective-permute-start | bytes 36872 | tf_op jit(solution)/shard_map/ppermute | solution.py:12
Sparse Core Ops, SparseCore 0:
  118.3 294.6 all-reduce.2
where the time goes:
time: 423 us; the launch traced here: 422 us
  waiting for transfers between devices  300 us (71%)
  starting transfers between devices  89.1 us (21%)
  between operations  14.6 us (3%)
  matrix products  11.5 us (3%)
    psum x1, waiting for transfers between devices, body(): summed_one, summed_two = lax.psum((grad_one, grad_two), ('lat', 'lon'))  291 us
    ppermute x8, starting transfers between devices, with_halo(): lax.ppermute(lax.slice_in_dim(block, 0, width, axis=dim), axis, backward)  48.2 us
    ppermute x8, starting transfers between devices, with_halo(): lax.ppermute(lax.slice_in_dim(block, block.shape[dim] - width, None, axis...  30.3 us
    ppermute x4, starting transfers between devices, shifted(): return lax.ppermute(block, axis, route)  10.5 us
  transfers between devices with their start and end apart: 21, of which 8 were waited for; matrix products, arithmetic and copies ran while one was open for 2% of the time, Pallas kernels for 0%

commit v1 on v0

--- a/solution.py
+++ b/solution.py
@@ -1,9 +1,15 @@
+import functools
 import math
 
 import jax
 import jax.numpy as jnp
 from jax import lax
+from jax.experimental import pallas as pl
+from jax.experimental.pallas import tpu as pltpu
 from jax.sharding import PartitionSpec as P
+
+MESH = pl.DeviceIdType.MESH
+RING = 8
 
 
 def shifted(block, axis, distance):
@@ -131,6 +137,212 @@
     return mirror_fix(heightened, 1)
 
 
+def coordinates():
+    lat = lax.axis_index("lat")
+    lon = lax.axis_index("lon")
+    core = lax.rem(lon, 2)
+    z = lax.rem(lax.div(lon, 2), RING)
+    x = lax.rem(lax.div(lon, 2 * RING), RING)
+    y = lat * 2 + lax.div(lon, 2 * RING * RING)
+    return core, x, y, z
+
+
+def device_at(core, x, y, z):
+    return (lax.div(y, 2), lax.rem(y, 2) * (2 * RING * RING) + x * (2 * RING) + z * 2 + core)
+
+
+def ring_peer(here, stage, step):
+    core, x, y, z = here
+    other = 1 - core
+    on_x, on_y, on_z = ((other, core, 0), (0, other, core), (core, 0, other))[stage]
+    return device_at(
+        core,
+        lax.rem(x + step * on_x, RING),
+        lax.rem(y + step * on_y, RING),
+        lax.rem(z + step * on_z, RING),
+    )
+
+
+def ring_index(here, stage):
+    core, x, y, z = here
+    first, second = ((x, y), (y, z), (z, x))[stage]
+    return first * (1 - core) + second * core
+
+
+def partner_of(here):
+    core, x, y, z = here
+    return device_at(1 - core, x, y, z)
+
+
+def greet_reducers(here, barrier):
+    pl.semaphore_signal(barrier, inc=1, device_id=partner_of(here), device_id_type=MESH)
+    for stage in range(3):
+
+        def greet(step, carry, stage=stage):
+            pl.semaphore_signal(
+                barrier, inc=1, device_id=ring_peer(here, stage, step), device_id_type=MESH
+            )
+            return carry
+
+        lax.fori_loop(1, RING, greet, 0)
+    return 1 + 3 * (RING - 1)
+
+
+def exchange(here, stage, source_of, landing, send_sem, recv_sem, arrived):
+    def copy(step):
+        return pltpu.make_async_remote_copy(
+            src_ref=source_of(step),
+            dst_ref=landing.at[step],
+            send_sem=send_sem.at[step],
+            recv_sem=recv_sem.at[step],
+            device_id=ring_peer(here, stage, step),
+            device_id_type=MESH,
+        )
+
+    def start(step, carry):
+        copy(step).start()
+        return carry
+
+    def finish(step, carry):
+        copy(step).wait_recv()
+        arrived(step)
+        return carry
+
+    def drain(step, carry):
+        copy(step).wait_send()
+        return carry
+
+    lax.fori_loop(1, RING, start, 0)
+    lax.fori_loop(1, RING, finish, 0)
+    lax.fori_loop(1, RING, drain, 0)
+
+
+def reduce_everywhere(here, terms, out_ref, scale, scratch):
+    (pair_out, pair_in, halves, wide_out, wide_in, narrow, narrow_out, narrow_in,
+     last, spread_in, chunk, own_half, other_half, pair_send, pair_recv, sends, recvs) = scratch
+    core = here[0]
+    pair_out[...] = terms[1 - core].astype(jnp.bfloat16)
+    swap = pltpu.make_async_remote_copy(
+        src_ref=pair_out, dst_ref=pair_in, send_sem=pair_send.at[0], recv_sem=pair_recv.at[0],
+        device_id=partner_of(here), device_id_type=MESH,
+    )
+    swap.start()
+    narrow[...] = jnp.zeros(narrow.shape, narrow.dtype)
+    swap.wait_recv()
+    halves[...] = terms[core] + pair_in[...].astype(jnp.float32)
+    wide_out[...] = halves[...].astype(jnp.bfloat16)
+
+    at_a, at_b, at_c = (ring_index(here, stage) for stage in range(3))
+    rows = halves.shape[1]
+    tile = narrow.shape[1]
+    own = narrow.at[: rows // tile]
+    own[...] = halves[at_a].reshape(rows // tile, tile, -1)
+
+    def add_wide(step):
+        own[...] += wide_in[step].astype(jnp.float32).reshape(rows // tile, tile, -1)
+
+    exchange(here, 0, lambda step: wide_out.at[lax.rem(at_a + step, RING)], wide_in,
+             sends.at[0], recvs.at[0], add_wide)
+    narrow_out[...] = narrow[...].astype(jnp.bfloat16)
+    last[0] = narrow[at_b]
+
+    def add_narrow(step):
+        last[0] += narrow_in[step].astype(jnp.float32)
+
+    exchange(here, 1, lambda step: narrow_out.at[lax.rem(at_b + step, RING)], narrow_in,
+             sends.at[1], recvs.at[1], add_narrow)
+    exchange(here, 2, lambda step: last.at[0], last, sends.at[2], recvs.at[2], lambda step: None)
+
+    total = last[at_c]
+    for source in range(1, RING):
+        total = total + last[lax.rem(at_c - source + RING, RING)]
+    spread_in[0] = (total * scale).astype(jnp.bfloat16)
+    exchange(here, 1, lambda step: spread_in.at[0], spread_in, sends.at[3], recvs.at[3],
+             lambda step: None)
+    for source in range(rows // tile):
+        chunk[0, source * tile : (source + 1) * tile] = spread_in[
+            lax.rem(at_b - source + RING, RING)
+        ]
+
+    def across(step):
+        return pltpu.make_async_remote_copy(
+            src_ref=chunk.at[step], dst_ref=other_half.at[step],
+            send_sem=pair_send.at[1 + step], recv_sem=pair_recv.at[1 + step],
+            device_id=partner_of(here), device_id_type=MESH,
+        )
+
+    across(0).start()
+    exchange(here, 0, lambda step: chunk.at[0], chunk, sends.at[4], recvs.at[4],
+             lambda step: across(step).start())
+    at_partner = at_a * 0 + here[2] * (1 - core) + here[1] * core
+
+    def place(source, carry):
+        out_ref[core, source] = chunk[lax.rem(at_a - source + RING, RING)]
+        return carry
+
+    lax.fori_loop(0, RING, place, 0)
+
+    def settle(step, carry):
+        across(step).wait()
+        return carry
+
+    lax.fori_loop(0, RING, settle, 0)
+
+    def place_other(source, carry):
+        out_ref[1 - core, source] = other_half[lax.rem(at_partner - source + RING, RING)]
+        return carry
+
+    lax.fori_loop(0, RING, place_other, 0)
+    swap.wait_send()
+
+
+def reduce_scratch(rows, lanes):
+    tile = 16
+    low, high = jnp.bfloat16, jnp.float32
+    return [
+        pltpu.VMEM((RING, rows, lanes), low),
+        pltpu.VMEM((RING, rows, lanes), low),
+        pltpu.VMEM((RING, rows, lanes), high),
+        pltpu.VMEM((RING, rows, lanes), low),
+        pltpu.VMEM((RING, rows, lanes), low),
+        pltpu.VMEM((RING, tile, lanes), high),
+        pltpu.VMEM((RING, tile, lanes), low),
+        pltpu.VMEM((RING, tile, lanes), low),
+        pltpu.VMEM((RING, tile, lanes), high),
+        pltpu.VMEM((RING, tile, lanes), low),
+        pltpu.VMEM((RING, rows, lanes), low),
+        pltpu.VMEM((RING, rows, lanes), low),
+        pltpu.VMEM((RING, rows, lanes), low),
+        pltpu.SemaphoreType.DMA((1 + RING,)),
+        pltpu.SemaphoreType.DMA((1 + RING,)),
+        pltpu.SemaphoreType.DMA((5, RING)),
+        pltpu.SemaphoreType.DMA((5, RING)),
+    ]
+
+
+def reduce_kernel(scale, terms_ref, out_ref, *scratch):
+    here = coordinates()
+    barrier = pltpu.get_barrier_semaphore()
+    pl.semaphore_wait(barrier, greet_reducers(here, barrier))
+    reduce_everywhere(here, terms_ref, out_ref, scale, scratch)
+
+
+def reduced(grad_one, grad_two, scale):
+    kernels, depth, lanes = grad_one.shape
+    rows = kernels * depth // RING
+    terms = jnp.stack([grad_one, grad_two]).reshape(2, RING, rows, lanes)
+    summed = pl.pallas_call(
+        functools.partial(reduce_kernel, scale),
+        out_shape=jax.ShapeDtypeStruct(terms.shape, jnp.bfloat16),
+        in_specs=[pl.BlockSpec(memory_space=pltpu.VMEM)],
+        out_specs=pl.BlockSpec(memory_space=pltpu.VMEM),
+        scratch_shapes=reduce_scratch(rows, lanes),
+        compiler_params=pltpu.CompilerParams(collective_id=0, has_side_effects=True),
+    )(terms)
+    summed = summed.astype(jnp.float32).reshape(2, kernels, depth, lanes)
+    return summed[0], summed[1]
+
+
 def body(fields, weight_one, weight_two, basis_raw, widths, cotangent):
     lat_count = fields.shape[0]
     lon_count = fields.shape[1]
@@ -163,9 +375,8 @@
     grad_one = weight_terms(u_one, dconv_one)
     du_one = mix_back(ext_one, weight_one)
     dfields = (dhidden + gather_back(du_one, source_rows(lat_count))).astype(jnp.bfloat16)
-    summed_one, summed_two = lax.psum((grad_one, grad_two), ("lat", "lon"))
     scale = 1.0 / math.sqrt(lat_count * lax.axis_size("lat") * lon_count * lax.axis_size("lon"))
-    return (output, dfields, summed_one * scale, summed_two * scale)
+    return (output, dfields, *reduced(grad_one, grad_two, scale))
 
 
 def solution(mesh):

time: 423 us -> 159 us (0.38)
  waiting for transfers between devices: 300 us -> 10.5 us
  Pallas kernels: 0 us -> 37.4 us
  between operations: 14.6 us -> 1.19 us
    psum x1 -> x0, waiting for transfers between devices: 291 us -> none  [body(): summed_one, summed_two = lax.psum((grad_one, grad_two), ('lat', 'lon'))]
    pallas_call x0 -> x1, Pallas kernels: none -> 37.4 us  [reduced(): pl.pallas_call(functools.partial(reduce_kernel, scale), out_shape=jax.Sha...]
    ppermute x8, waiting for transfers between devices: 8.14 us -> 1.51 us  [with_halo(): lax.ppermute(lax.slice_in_dim(block, 0, width, axis=dim), axis, backward)]
    ppermute x8, waiting for transfers between devices: 0.02 us -> 4.39 us  [with_halo(): lax.ppermute(lax.slice_in_dim(block, block.shape[dim] - width, None, axis...]
  transfers between devices with their start and end apart: 21 -> 20, of which waited for: 8 -> 8; matrix products, arithmetic and copies ran while one was open for 2% -> 6% of each run, Pallas kernels for 0% -> 24%
where the time goes in v1:
time: 159 us; the launch traced here: 157 us
  starting transfers between devices  88.6 us (56%)
  Pallas kernels  37.4 us (24%)
  matrix products  10.6 us (7%)
  waiting for transfers between devices  10.5 us (7%)
  local copies, waits for them, and re-layouts  5.7 us (4%)
  other arithmetic  2.82 us (2%)
    ppermute x8, starting transfers between devices, with_halo(): lax.ppermute(lax.slice_in_dim(block, 0, width, axis=dim), axis, backward)  50.9 us
    pallas_call x1, Pallas kernels, reduced(): pl.pallas_call(functools.partial(reduce_kernel, scale), out_shape=jax.Sha...  37.4 us
    ppermute x8, starting transfers between devices, with_halo(): lax.ppermute(lax.slice_in_dim(block, block.shape[dim] - width, None, axis...  28.7 us
    ppermute x4, starting transfers between devices, shifted(): return lax.ppermute(block, axis, route)  8.91 us
    ppermute x4, waiting for transfers between devices, shifted(): return lax.ppermute(block, axis, route)  4.64 us
    ppermute x8, waiting for transfers between devices, with_halo(): lax.ppermute(lax.slice_in_dim(block, block.shape[dim] - width, None, axis...  4.39 us
    dot_general x6, matrix products, gather_back(): jnp.einsum('kjlm,jmkc->jlc', band_rows, extended[first_tap:first_tap + ro...  3.6 us
  transfers between devices with their start and end apart: 20, of which 8 were waited for; matrix products, arithmetic and copies ran while one was open for 6% of the time, Pallas kernels for 24%

profile of v1, /device:TPU:1, one launch (start us, length us, event | category | flops | bytes accessed | tf_op | source)
XLA Modules:
  0.0 156.8 jit_solution(12164752532700205458)
XLA Ops:
  0.6 0.8 fusion.118
  1.5 16.1 %collective-permute-start.1 = (bf16[16,4,128]{2,1,0:T(4,128)(2,1)S(1)}, bf16[16,4,128]{2,1,0:T(4,128)(2,1)S(1)}, u32[]{:S(2)}, u32[]{:S(2)}) collective-permute-start(bf16[16,4,128]{2,1,0:T(4,128)(2,1)S(1)} %get-tuple-element.23), channel_id=1, source_target_pairs={{1,0},{2,1},{3,2},{4,3},{5,4},{6,5},{7,6},{8,7},{9,8},{10,9},{11,1... | collective-permute-start | bytes 49160 | tf_op jit(solution)/shard_map/ppermute | solution.py:31
  17.6 1.9 %collective-permute-start = (bf16[16,4,128]{2,1,0:T(4,128)(2,1)S(1)}, bf16[16,4,128]{2,1,0:T(4,128)(2,1)S(1)}, u32[]{:S(2)}, u32[]{:S(2)}) collective-permute-start(bf16[16,4,128]{2,1,0:T(4,128)(2,1)S(1)} %get-tuple-element.22), channel_id=1, source_target_pairs={{0,1},{1,2},{2,3},{3,4},{4,5},{5,6},{6,7},{7,8},{8,9},{9,10},{10,1... | collective-permute-start | bytes 49160 | tf_op jit(solution)/shard_map/ppermute | solution.py:28
  19.5 0.7 compare_convert_fusion
  20.3 0.8 broadcast_multiply_fusion
  21.2 0.2 concatenate.51
  21.5 0.1 copy.69
  21.8 0.3 convolution_convert_fusion.6
  22.1 0.3 convolution_convert_fusion.7
  22.4 0.1 copy.70
  22.6 0.3 convolution_convert_fusion.5
  23.1 0.3 convolution_convert_fusion.2
  23.5 0.1 copy.73
  23.6 2.2 %collective-permute-done = bf16[16,4,128]{2,1,0:T(4,128)(2,1)S(1)} collective-permute-done((bf16[16,4,128]{2,1,0:T(4,128)(2,1)S(1)}, bf16[16,4,128]{2,1,0:T(4,128)(2,1)S(1)}, u32[]{:S(2)}, u32[]{:S(2)}) %collective-permute-start) | collective-permute-done | bytes 16416 | tf_op jit(solution)/shard_map/ppermute | solution.py:28
  25.8 1.3 collective-permute-start.4
  27.1 5.1 %collective-permute-start.3 = (bf16[1,24,128]{2,1,0:T(8,128)(2,1)S(1)}, bf16[1,24,128]{2,1,0:T(8,128)(2,1)S(1)}, u32[]{:S(2)}, u32[]{:S(2)}) collective-permute-start(bf16[1,24,128]{2,1,0:T(8,128)(2,1)S(1)} %get-tuple-element.15), channel_id=1, source_target_pairs={{0,256},{256,512},{512,768},{1,257},{257,513},{513,769},{2,258},{2... | collective-permute-start | bytes 18440 | tf_op jit(solution)/shard_map/ppermute | solution.py:28
  32.2 2.0 %collective-permute-start.2 = (bf16[2,24,128]{2,1,0:T(8,128)(2,1)S(1)}, bf16[2,24,128]{2,1,0:T(8,128)(2,1)S(1)}, u32[]{:S(2)}, u32[]{:S(2)}) collective-permute-start(bf16[2,24,128]{2,1,0:T(8,128)(2,1)S(1)} %pad_maximum_fusion.23), channel_id=1, source_target_pairs={{128,0},{129,1},{130,2},{131,3},{132,4},{133,5},{134,6},{135,7},{1... | collective-permute-start | bytes 36872 | tf_op jit(solution)/shard_map/ppermute | solution.py:18
  34.2 0.3 fusion.27
  34.5 2.2 %collective-permute-done.2 = bf16[2,24,128]{2,1,0:T(8,128)(2,1)S(1)} collective-permute-done((bf16[2,24,128]{2,1,0:T(8,128)(2,1)S(1)}, bf16[2,24,128]{2,1,0:T(8,128)(2,1)S(1)}, u32[]{:S(2)}, u32[]{:S(2)}) %collective-permute-start.2) | collective-permute-done | bytes 12320 | tf_op jit(solution)/shard_map/ppermute | solution.py:18
  36.7 0.3 convolution_add_fusion.3
  37.0 0.3 fusion.3
  37.2 0.6 copy-done.2
  37.9 0.9 add_convert_fusion.1
  38.8 10.1 %collective-permute-start.6 = (bf16[16,4,128]{2,1,0:T(4,128)(2,1)S(1)}, bf16[16,4,128]{2,1,0:T(4,128)(2,1)S(1)}, u32[]{:S(2)}, u32[]{:S(2)}) collective-permute-start(bf16[16,4,128]{2,1,0:T(4,128)(2,1)S(1)} %get-tuple-element.21), channel_id=1, source_target_pairs={{1,0},{2,1},{3,2},{4,3},{5,4},{6,5},{7,6},{8,7},{9,8},{10,9},{11,1... | collective-permute-start | bytes 49160 | tf_op jit(solution)/shard_map/ppermute | solution.py:31
  49.0 1.9 %collective-permute-start.5 = (bf16[16,4,128]{2,1,0:T(4,128)(2,1)S(1)}, bf16[16,4,128]{2,1,0:T(4,128)(2,1)S(1)}, u32[]{:S(2)}, u32[]{:S(2)}) collective-permute-start(bf16[16,4,128]{2,1,0:T(4,128)(2,1)S(1)} %get-tuple-element.20), channel_id=1, source_target_pairs={{0,1},{1,2},{2,3},{3,4},{4,5},{5,6},{6,7},{7,8},{8,9},{9,10},{10,1... | collective-permute-start | bytes 49160 | tf_op jit(solution)/shard_map/ppermute | solution.py:28
  50.9 0.3 convolution_convert_fusion.3
  51.4 1.4 collective-permute-done.5
  52.8 1.3 collective-permute-start.9
  54.1 6.1 %collective-permute-start.8 = (bf16[1,24,128]{2,1,0:T(8,128)(2,1)S(1)}, bf16[1,24,128]{2,1,0:T(8,128)(2,1)S(1)}, u32[]{:S(2)}, u32[]{:S(2)}) collective-permute-start(bf16[1,24,128]{2,1,0:T(8,128)(2,1)S(1)} %get-tuple-element.13), channel_id=1, source_target_pairs={{0,256},{256,512},{512,768},{1,257},{257,513},{513,769},{2,258},{2... | collective-permute-start | bytes 18440 | tf_op jit(solution)/shard_map/ppermute | solution.py:28
  60.2 2.2 %collective-permute-start.7 = (bf16[2,24,128]{2,1,0:T(8,128)(2,1)S(1)}, bf16[2,24,128]{2,1,0:T(8,128)(2,1)S(1)}, u32[]{:S(2)}, u32[]{:S(2)}) collective-permute-start(bf16[2,24,128]{2,1,0:T(8,128)(2,1)S(1)} %pad_maximum_fusion.24), channel_id=1, source_target_pairs={{128,0},{129,1},{130,2},{131,3},{132,4},{133,5},{134,6},{135,7},{1... | collective-permute-start | bytes 36872 | tf_op jit(solution)/shard_map/ppermute | solution.py:18
  62.4 0.3 fusion.25
  62.7 2.0 %collective-permute-done.7 = bf16[2,24,128]{2,1,0:T(8,128)(2,1)S(1)} collective-permute-done((bf16[2,24,128]{2,1,0:T(8,128)(2,1)S(1)}, bf16[2,24,128]{2,1,0:T(8,128)(2,1)S(1)}, u32[]{:S(2)}, u32[]{:S(2)}) %collective-permute-start.7) | collective-permute-done | bytes 12320 | tf_op jit(solution)/shard_map/ppermute | solution.py:18
  64.7 0.3 convolution_add_fusion.1
  65.0 0.3 fusion.2
  65.3 0.5 copy-done.3
  65.8 1.0 fusion.48
  66.8 10.0 %collective-permute-start.11 = (bf16[16,4,128]{2,1,0:T(4,128)(2,1)S(1)}, bf16[16,4,128]{2,1,0:T(4,128)(2,1)S(1)}, u32[]{:S(2)}, u32[]{:S(2)}) collective-permute-start(bf16[16,4,128]{2,1,0:T(4,128)(2,1)S(1)} %get-tuple-element.19), channel_id=1, source_target_pairs={{1,0},{2,1},{3,2},{4,3},{5,4},{6,5},{7,6},{8,7},{9,8},{10,9},{11,1... | collective-permute-start | bytes 49160 | tf_op jit(solution)/shard_map/ppermute | solution.py:31
  76.9 1.9 %collective-permute-start.10 = (bf16[16,4,128]{2,1,0:T(4,128)(2,1)S(1)}, bf16[16,4,128]{2,1,0:T(4,128)(2,1)S(1)}, u32[]{:S(2)}, u32[]{:S(2)}) collective-permute-start(bf16[16,4,128]{2,1,0:T(4,128)(2,1)S(1)} %get-tuple-element.18), channel_id=1, source_target_pairs={{0,1},{1,2},{2,3},{3,4},{4,5},{5,6},{6,7},{7,8},{8,9},{9,10},{10,1... | collective-permute-start | bytes 49160 | tf_op jit(solution)/shard_map/ppermute | solution.py:28
  78.8 0.3 convolution_convert_fusion.4
  79.1 0.8 collective-permute-done.10
  80.0 5.8 %collective-permute-start.13 = (bf16[1,24,128]{2,1,0:T(8,128)(2,1)S(1)}, bf16[1,24,128]{2,1,0:T(8,128)(2,1)S(1)}, u32[]{:S(2)}, u32[]{:S(2)}) collective-permute-start(bf16[1,24,128]{2,1,0:T(8,128)(2,1)S(1)} %get-tuple-element.10), channel_id=1, source_target_pairs={{0,256},{256,512},{512,768},{1,257},{257,513},{513,769},{2,258},{2... | collective-permute-start | bytes 18440 | tf_op jit(solution)/shard_map/ppermute | solution.py:28
  85.7 1.3 collective-permute-start.14
  87.0 2.2 %collective-permute-start.12 = (bf16[2,24,128]{2,1,0:T(8,128)(2,1)S(1)}, bf16[2,24,128]{2,1,0:T(8,128)(2,1)S(1)}, u32[]{:S(2)}, u32[]{:S(2)}) collective-permute-start(bf16[2,24,128]{2,1,0:T(8,128)(2,1)S(1)} %pad_maximum_fusion.25), channel_id=1, source_target_pairs={{128,0},{129,1},{130,2},{131,3},{132,4},{133,5},{134,6},{135,7},{1... | collective-permute-start | bytes 36872 | tf_op jit(solution)/shard_map/ppermute | solution.py:18
  89.2 0.3 fusion.90
  89.5 1.5 collective-permute-done.14
  91.0 0.4 collective-permute-done.12
  91.5 0.4 convolution_convert_fusion.1
  91.9 0.5 convolution_bitcast_fusion.3
  92.4 0.5 convolution_bitcast_fusion.4
  92.9 0.4 copy-done.4
  93.3 0.5 fusion.41
  93.8 0.3 fusion.92
  94.2 9.5 %collective-permute-start.16 = (bf16[16,4,128]{2,1,0:T(4,128)(2,1)S(1)}, bf16[16,4,128]{2,1,0:T(4,128)(2,1)S(1)}, u32[]{:S(2)}, u32[]{:S(2)}) collective-permute-start(bf16[16,4,128]{2,1,0:T(4,128)(2,1)S(1)} %get-tuple-element.17), channel_id=1, source_target_pairs={{1,0},{2,1},{3,2},{4,3},{5,4},{6,5},{7,6},{8,7},{9,8},{10,9},{11,1... | collective-permute-start | bytes 49160 | tf_op jit(solution)/shard_map/ppermute | solution.py:31
  103.7 1.9 %collective-permute-start.15 = (bf16[16,4,128]{2,1,0:T(4,128)(2,1)S(1)}, bf16[16,4,128]{2,1,0:T(4,128)(2,1)S(1)}, u32[]{:S(2)}, u32[]{:S(2)}) collective-permute-start(bf16[16,4,128]{2,1,0:T(4,128)(2,1)S(1)} %get-tuple-element.16), channel_id=1, source_target_pairs={{0,1},{1,2},{2,3},{3,4},{4,5},{5,6},{6,7},{7,8},{8,9},{9,10},{10,1... | collective-permute-start | bytes 49160 | tf_op jit(solution)/shard_map/ppermute | solution.py:28
  105.7 1.0 pad_maximum_fusion.terms_ref
  106.7 37.4 %shard_map.93 = bf16[2,8,112,128]{3,2,1,0:T(8,128)(2,1)} custom-call(f32[2,8,112,128]{3,2,1,0:T(8,128)} %pad_maximum_fusion.terms_ref), custom_call_target="tpu_custom_call" | custom-call | tf_op jit(solution)/shard_map/pallas_call | solution.py:334
  144.1 4.1 %collective-permute-start.18 = (bf16[1,24,128]{2,1,0:T(8,128)(2,1)S(1)}, bf16[1,24,128]{2,1,0:T(8,128)(2,1)S(1)}, u32[]{:S(2)}, u32[]{:S(2)}) collective-permute-start(bf16[1,24,128]{2,1,0:T(8,128)(2,1)S(1)} %get-tuple-element.8), channel_id=1, source_target_pairs={{0,256},{256,512},{512,768},{1,257},{257,513},{513,769},{2,258},{2... | collective-permute-start | bytes 18440 | tf_op jit(solution)/shard_map/ppermute | solution.py:28
  148.2 1.3 collective-permute-start.19
  149.5 2.6 %collective-permute-start.17 = (bf16[2,24,128]{2,1,0:T(8,128)(2,1)S(1)}, bf16[2,24,128]{2,1,0:T(8,128)(2,1)S(1)}, u32[]{:S(2)}, u32[]{:S(2)}) collective-permute-start(bf16[2,24,128]{2,1,0:T(8,128)(2,1)S(1)} %pad_maximum_fusion.26), channel_id=1, source_target_pairs={{128,0},{129,1},{130,2},{131,3},{132,4},{133,5},{134,6},{135,7},{1... | collective-permute-start | bytes 36872 | tf_op jit(solution)/shard_map/ppermute | solution.py:18
  152.2 2.0 %fusion.112 = (f32[1,8,112,128]{3,2,1,0:T(8,128)}, f32[1,8,112,128]{3,2,1,0:T(8,128)}) fusion(bf16[2,8,112,128]{3,2,1,0:T(8,128)(2,1)} %shard_map.93), kind=kLoop, calls=%fused_computation.179 | loop fusion | bytes 1835008 | tf_op jit(solution)/shard_map/slice | solution.py:343
  154.3 0.4 convolution_convert_fusion
  154.7 0.5 convolution_bitcast_fusion
  155.2 0.5 convolution_bitcast_fusion.1
  155.7 1.1 fusion.10
  (49 shorter events, 1.0 us)
Async XLA Ops:
  0.6 64.6 %copy-start = (bf16[7,128,128]{2,1,0:T(8,128)(2,1)S(1)}, bf16[7,128,128]{2,1,0:T(8,128)(2,1)}, u32[]{:S(2)}) copy-start(bf16[7,128,128]{2,1,0:T(8,128)(2,1)} %param.8) | copy-start | bytes 688132
  1.5 22.1 %collective-permute-start.1 = (bf16[16,4,128]{2,1,0:T(4,128)(2,1)S(1)}, bf16[16,4,128]{2,1,0:T(4,128)(2,1)S(1)}, u32[]{:S(2)}, u32[]{:S(2)}) collective-permute-start(bf16[16,4,128]{2,1,0:T(4,128)(2,1)S(1)} %get-tuple-element.23), channel_id=1, source_target_pairs={{1,0},{2,1},{3,2},{4,3},{5,4},{6,5},{7,6},{8,7},{9,8},{10,9},{11,1... | collective-permute-start | bytes 49160 | tf_op jit(solution)/shard_map/ppermute | solution.py:31
  17.6 8.2 %collective-permute-start = (bf16[16,4,128]{2,1,0:T(4,128)(2,1)S(1)}, bf16[16,4,128]{2,1,0:T(4,128)(2,1)S(1)}, u32[]{:S(2)}, u32[]{:S(2)}) collective-permute-start(bf16[16,4,128]{2,1,0:T(4,128)(2,1)S(1)} %get-tuple-element.22), channel_id=1, source_target_pairs={{0,1},{1,2},{2,3},{3,4},{4,5},{5,6},{6,7},{7,8},{8,9},{9,10},{10,1... | collective-permute-start | bytes 49160 | tf_op jit(solution)/shard_map/ppermute | solution.py:28
  22.1 3.7 %copy-start.1 = (bf16[16,16,128]{2,1,0:T(8,128)(2,1)S(1)}, bf16[16,16,128]{2,1,0:T(8,128)(2,1)}, u32[]{:S(2)}) copy-start(bf16[16,16,128]{2,1,0:T(8,128)(2,1)} %param.6) | copy-start | bytes 196612
  25.8 8.6 %collective-permute-start.4 = (bf16[1,24,128]{2,1,0:T(8,128)(2,1)S(1)}, bf16[1,24,128]{2,1,0:T(8,128)(2,1)S(1)}, u32[]{:S(2)}, u32[]{:S(2)}) collective-permute-start(bf16[1,24,128]{2,1,0:T(8,128)(2,1)S(1)} %get-tuple-element.14), channel_id=1, source_target_pairs={{256,0},{512,256},{768,512},{257,1},{513,257},{769,513},{258,2},{5... | collective-permute-start | bytes 18440 | tf_op jit(solution)/shard_map/ppermute | solution.py:31
  27.1 7.3 %collective-permute-start.3 = (bf16[1,24,128]{2,1,0:T(8,128)(2,1)S(1)}, bf16[1,24,128]{2,1,0:T(8,128)(2,1)S(1)}, u32[]{:S(2)}, u32[]{:S(2)}) collective-permute-start(bf16[1,24,128]{2,1,0:T(8,128)(2,1)S(1)} %get-tuple-element.15), channel_id=1, source_target_pairs={{0,256},{256,512},{512,768},{1,257},{257,513},{513,769},{2,258},{2... | collective-permute-start | bytes 18440 | tf_op jit(solution)/shard_map/ppermute | solution.py:28
  32.2 4.4 %collective-permute-start.2 = (bf16[2,24,128]{2,1,0:T(8,128)(2,1)S(1)}, bf16[2,24,128]{2,1,0:T(8,128)(2,1)S(1)}, u32[]{:S(2)}, u32[]{:S(2)}) collective-permute-start(bf16[2,24,128]{2,1,0:T(8,128)(2,1)S(1)} %pad_maximum_fusion.23), channel_id=1, source_target_pairs={{128,0},{129,1},{130,2},{131,3},{132,4},{133,5},{134,6},{135,7},{1... | collective-permute-start | bytes 36872 | tf_op jit(solution)/shard_map/ppermute | solution.py:18
  36.9 0.9 copy-start.2
  38.8 12.5 %collective-permute-start.6 = (bf16[16,4,128]{2,1,0:T(4,128)(2,1)S(1)}, bf16[16,4,128]{2,1,0:T(4,128)(2,1)S(1)}, u32[]{:S(2)}, u32[]{:S(2)}) collective-permute-start(bf16[16,4,128]{2,1,0:T(4,128)(2,1)S(1)} %get-tuple-element.21), channel_id=1, source_target_pairs={{1,0},{2,1},{3,2},{4,3},{5,4},{6,5},{7,6},{8,7},{9,8},{10,9},{11,1... | collective-permute-start | bytes 49160 | tf_op jit(solution)/shard_map/ppermute | solution.py:31
  49.0 3.8 %collective-permute-start.5 = (bf16[16,4,128]{2,1,0:T(4,128)(2,1)S(1)}, bf16[16,4,128]{2,1,0:T(4,128)(2,1)S(1)}, u32[]{:S(2)}, u32[]{:S(2)}) collective-permute-start(bf16[16,4,128]{2,1,0:T(4,128)(2,1)S(1)} %get-tuple-element.20), channel_id=1, source_target_pairs={{0,1},{1,2},{2,3},{3,4},{4,5},{5,6},{6,7},{7,8},{8,9},{9,10},{10,1... | collective-permute-start | bytes 49160 | tf_op jit(solution)/shard_map/ppermute | solution.py:28
  52.8 9.9 %collective-permute-start.9 = (bf16[1,24,128]{2,1,0:T(8,128)(2,1)S(1)}, bf16[1,24,128]{2,1,0:T(8,128)(2,1)S(1)}, u32[]{:S(2)}, u32[]{:S(2)}) collective-permute-start(bf16[1,24,128]{2,1,0:T(8,128)(2,1)S(1)} %get-tuple-element.12), channel_id=1, source_target_pairs={{256,0},{512,256},{768,512},{257,1},{513,257},{769,513},{258,2},{5... | collective-permute-start | bytes 18440 | tf_op jit(solution)/shard_map/ppermute | solution.py:31
  54.1 8.6 %collective-permute-start.8 = (bf16[1,24,128]{2,1,0:T(8,128)(2,1)S(1)}, bf16[1,24,128]{2,1,0:T(8,128)(2,1)S(1)}, u32[]{:S(2)}, u32[]{:S(2)}) collective-permute-start(bf16[1,24,128]{2,1,0:T(8,128)(2,1)S(1)} %get-tuple-element.13), channel_id=1, source_target_pairs={{0,256},{256,512},{512,768},{1,257},{257,513},{513,769},{2,258},{2... | collective-permute-start | bytes 18440 | tf_op jit(solution)/shard_map/ppermute | solution.py:28
  60.2 4.4 %collective-permute-start.7 = (bf16[2,24,128]{2,1,0:T(8,128)(2,1)S(1)}, bf16[2,24,128]{2,1,0:T(8,128)(2,1)S(1)}, u32[]{:S(2)}, u32[]{:S(2)}) collective-permute-start(bf16[2,24,128]{2,1,0:T(8,128)(2,1)S(1)} %pad_maximum_fusion.24), channel_id=1, source_target_pairs={{128,0},{129,1},{130,2},{131,3},{132,4},{133,5},{134,6},{135,7},{1... | collective-permute-start | bytes 36872 | tf_op jit(solution)/shard_map/ppermute | solution.py:18
  65.0 0.8 copy-start.3
  66.8 12.3 %collective-permute-start.11 = (bf16[16,4,128]{2,1,0:T(4,128)(2,1)S(1)}, bf16[16,4,128]{2,1,0:T(4,128)(2,1)S(1)}, u32[]{:S(2)}, u32[]{:S(2)}) collective-permute-start(bf16[16,4,128]{2,1,0:T(4,128)(2,1)S(1)} %get-tuple-element.19), channel_id=1, source_target_pairs={{1,0},{2,1},{3,2},{4,3},{5,4},{6,5},{7,6},{8,7},{9,8},{10,9},{11,1... | collective-permute-start | bytes 49160 | tf_op jit(solution)/shard_map/ppermute | solution.py:31
  76.9 3.1 %collective-permute-start.10 = (bf16[16,4,128]{2,1,0:T(4,128)(2,1)S(1)}, bf16[16,4,128]{2,1,0:T(4,128)(2,1)S(1)}, u32[]{:S(2)}, u32[]{:S(2)}) collective-permute-start(bf16[16,4,128]{2,1,0:T(4,128)(2,1)S(1)} %get-tuple-element.18), channel_id=1, source_target_pairs={{0,1},{1,2},{2,3},{3,4},{4,5},{5,6},{6,7},{7,8},{8,9},{9,10},{10,1... | collective-permute-start | bytes 49160 | tf_op jit(solution)/shard_map/ppermute | solution.py:28
  80.0 9.6 %collective-permute-start.13 = (bf16[1,24,128]{2,1,0:T(8,128)(2,1)S(1)}, bf16[1,24,128]{2,1,0:T(8,128)(2,1)S(1)}, u32[]{:S(2)}, u32[]{:S(2)}) collective-permute-start(bf16[1,24,128]{2,1,0:T(8,128)(2,1)S(1)} %get-tuple-element.10), channel_id=1, source_target_pairs={{0,256},{256,512},{512,768},{1,257},{257,513},{513,769},{2,258},{2... | collective-permute-start | bytes 18440 | tf_op jit(solution)/shard_map/ppermute | solution.py:28
  85.7 5.3 %collective-permute-start.14 = (bf16[1,24,128]{2,1,0:T(8,128)(2,1)S(1)}, bf16[1,24,128]{2,1,0:T(8,128)(2,1)S(1)}, u32[]{:S(2)}, u32[]{:S(2)}) collective-permute-start(bf16[1,24,128]{2,1,0:T(8,128)(2,1)S(1)} %get-tuple-element.11), channel_id=1, source_target_pairs={{256,0},{512,256},{768,512},{257,1},{513,257},{769,513},{258,2},{5... | collective-permute-start | bytes 18440 | tf_op jit(solution)/shard_map/ppermute | solution.py:31
  87.0 4.4 %collective-permute-start.12 = (bf16[2,24,128]{2,1,0:T(8,128)(2,1)S(1)}, bf16[2,24,128]{2,1,0:T(8,128)(2,1)S(1)}, u32[]{:S(2)}, u32[]{:S(2)}) collective-permute-start(bf16[2,24,128]{2,1,0:T(8,128)(2,1)S(1)} %pad_maximum_fusion.25), channel_id=1, source_target_pairs={{128,0},{129,1},{130,2},{131,3},{132,4},{133,5},{134,6},{135,7},{1... | collective-permute-start | bytes 36872 | tf_op jit(solution)/shard_map/ppermute | solution.py:18
  92.4 0.9 copy-start.4
  94.2 49.9 %collective-permute-start.16 = (bf16[16,4,128]{2,1,0:T(4,128)(2,1)S(1)}, bf16[16,4,128]{2,1,0:T(4,128)(2,1)S(1)}, u32[]{:S(2)}, u32[]{:S(2)}) collective-permute-start(bf16[16,4,128]{2,1,0:T(4,128)(2,1)S(1)} %get-tuple-element.17), channel_id=1, source_target_pairs={{1,0},{2,1},{3,2},{4,3},{5,4},{6,5},{7,6},{8,7},{9,8},{10,9},{11,1... | collective-permute-start | bytes 49160 | tf_op jit(solution)/shard_map/ppermute | solution.py:31
  103.7 40.3 %collective-permute-start.15 = (bf16[16,4,128]{2,1,0:T(4,128)(2,1)S(1)}, bf16[16,4,128]{2,1,0:T(4,128)(2,1)S(1)}, u32[]{:S(2)}, u32[]{:S(2)}) collective-permute-start(bf16[16,4,128]{2,1,0:T(4,128)(2,1)S(1)} %get-tuple-element.16), channel_id=1, source_target_pairs={{0,1},{1,2},{2,3},{3,4},{4,5},{5,6},{6,7},{7,8},{8,9},{9,10},{10,1... | collective-permute-start | bytes 49160 | tf_op jit(solution)/shard_map/ppermute | solution.py:28
  144.1 10.1 %collective-permute-start.18 = (bf16[1,24,128]{2,1,0:T(8,128)(2,1)S(1)}, bf16[1,24,128]{2,1,0:T(8,128)(2,1)S(1)}, u32[]{:S(2)}, u32[]{:S(2)}) collective-permute-start(bf16[1,24,128]{2,1,0:T(8,128)(2,1)S(1)} %get-tuple-element.8), channel_id=1, source_target_pairs={{0,256},{256,512},{512,768},{1,257},{257,513},{513,769},{2,258},{2... | collective-permute-start | bytes 18440 | tf_op jit(solution)/shard_map/ppermute | solution.py:28
  148.2 6.0 %collective-permute-start.19 = (bf16[1,24,128]{2,1,0:T(8,128)(2,1)S(1)}, bf16[1,24,128]{2,1,0:T(8,128)(2,1)S(1)}, u32[]{:S(2)}, u32[]{:S(2)}) collective-permute-start(bf16[1,24,128]{2,1,0:T(8,128)(2,1)S(1)} %get-tuple-element.9), channel_id=1, source_target_pairs={{256,0},{512,256},{768,512},{257,1},{513,257},{769,513},{258,2},{5... | collective-permute-start | bytes 18440 | tf_op jit(solution)/shard_map/ppermute | solution.py:31
  149.5 4.7 %collective-permute-start.17 = (bf16[2,24,128]{2,1,0:T(8,128)(2,1)S(1)}, bf16[2,24,128]{2,1,0:T(8,128)(2,1)S(1)}, u32[]{:S(2)}, u32[]{:S(2)}) collective-permute-start(bf16[2,24,128]{2,1,0:T(8,128)(2,1)S(1)} %pad_maximum_fusion.26), channel_id=1, source_target_pairs={{128,0},{129,1},{130,2},{131,3},{132,4},{133,5},{134,6},{135,7},{1... | collective-permute-start | bytes 36872 | tf_op jit(solution)/shard_map/ppermute | solution.py:18

commit v2 on v1

v2 whole, which is shorter than its diff:
```python
import functools
import math

import jax
import jax.numpy as jnp
from jax import lax
from jax.experimental import pallas as pl
from jax.experimental.pallas import tpu as pltpu
from jax.sharding import PartitionSpec as P

MESH = pl.DeviceIdType.MESH
RING = 8
RIM = 8
LANES = 128
GELU_SLOPE = math.sqrt(2.0 / math.pi)
GELU_CUBIC = 0.044715


def padded_basis(basis_raw, widths):
    tap_count = basis_raw.shape[3]
    reach = (tap_count - 1) // 2
    distance = jnp.abs(jnp.arange(tap_count, dtype=jnp.int32) - reach)
    inside = (distance[None, :] <= widths[:, None]).astype(jnp.bfloat16)
    masked = basis_raw * inside[None, :, None, :]
    top_rows = masked[:, 0:1, ::-1, :]
    bottom = masked[:, -1:, ::-1, :]
    zero_row = jnp.zeros_like(top_rows)
    return jnp.concatenate([zero_row, top_rows, masked, bottom, zero_row], axis=1)


def coordinates():
    lat = lax.axis_index("lat")
    lon = lax.axis_index("lon")
    core = lax.rem(lon, 2)
    z = lax.rem(lax.div(lon, 2), RING)
    x = lax.rem(lax.div(lon, 2 * RING), RING)
    y = lat * 2 + lax.div(lon, 2 * RING * RING)
    return core, x, y, z


def device_at(core, x, y, z):
    return (lax.div(y, 2), lax.rem(y, 2) * (2 * RING * RING) + x * (2 * RING) + z * 2 + core)


def ring_peer(here, stage, step):
    core, x, y, z = here
    other = 1 - core
    on_x, on_y, on_z = ((other, core, 0), (0, other, core), (core, 0, other))[stage]
    return device_at(
        core,
        lax.rem(x + step * on_x, RING),
        lax.rem(y + step * on_y, RING),
        lax.rem(z + step * on_z, RING),
    )


def ring_index(here, stage):
    core, x, y, z = here
    first, second = ((x, y), (y, z), (z, x))[stage]
    return first * (1 - core) + second * core


def partner_of(here):
    core, x, y, z = here
    return device_at(1 - core, x, y, z)


def greet_reducers(here, barrier):
    pl.semaphore_signal(barrier, inc=1, device_id=partner_of(here), device_id_type=MESH)
    for stage in range(3):

        def greet(step, carry, stage=stage):
            pl.semaphore_signal(
                barrier, inc=1, device_id=ring_peer(here, stage, step), device_id_type=MESH
            )
            return carry

        lax.fori_loop(1, RING, greet, 0)
    return 1 + 3 * (RING - 1)


def exchange(here, stage, source_of, landing, send_sem, recv_sem, arrived, meanwhile=None):
    def copy(step):
        return pltpu.make_async_remote_copy(
            src_ref=source_of(step),
            dst_ref=landing.at[step],
            send_sem=send_sem.at[step],
            recv_sem=recv_sem.at[step],
            device_id=ring_peer(here, stage, step),
            device_id_type=MESH,
        )

    def start(step, carry):
        copy(step).start()
        return carry

    def finish(step, carry):
        copy(step).wait_recv()
        arrived(step)
        return carry

    def drain(step, carry):
        copy(step).wait_send()
        return carry

    lax.fori_loop(1, RING, start, 0)
    if meanwhile is not None:
        meanwhile()
    lax.fori_loop(1, RING, finish, 0)
    lax.fori_loop(1, RING, drain, 0)


def reduce_everywhere(here, terms, out_ref, scale, scratch, meanwhile):
    (pair_out, pair_in, halves, wide_out, wide_in, narrow, narrow_out, narrow_in,
     last, spread_in, chunk, own_half, other_half, pair_send, pair_recv, sends, recvs) = scratch
    core = here[0]
    pair_out[...] = terms[1 - core].astype(jnp.bfloat16)
    swap = pltpu.make_async_remote_copy(
        src_ref=pair_out, dst_ref=pair_in, send_sem=pair_send.at[0], recv_sem=pair_recv.at[0],
        device_id=partner_of(here), device_id_type=MESH,
    )
    swap.start()
    narrow[...] = jnp.zeros(narrow.shape, narrow.dtype)
    swap.wait_recv()
    halves[...] = terms[core] + pair_in[...].astype(jnp.float32)
    wide_out[...] = halves[...].astype(jnp.bfloat16)

    at_a, at_b, at_c = (ring_index(here, stage) for stage in range(3))
    rows = halves.shape[1]
    tile = narrow.shape[1]
    own = narrow.at[: rows // tile]
    own[...] = halves[at_a].reshape(rows // tile, tile, -1)

    def add_wide(step):
        own[...] += wide_in[step].astype(jnp.float32).reshape(rows // tile, tile, -1)

    exchange(here, 0, lambda step: wide_out.at[lax.rem(at_a + step, RING)], wide_in,
             sends.at[0], recvs.at[0], add_wide, meanwhile)
    narrow_out[...] = narrow[...].astype(jnp.bfloat16)
    last[0] = narrow[at_b]

    def add_narrow(step):
        last[0] += narrow_in[step].astype(jnp.float32)

    exchange(here, 1, lambda step: narrow_out.at[lax.rem(at_b + step, RING)], narrow_in,
             sends.at[1], recvs.at[1], add_narrow)
    exchange(here, 2, lambda step: last.at[0], last, sends.at[2], recvs.at[2], lambda step: None)

    total = last[at_c]
    for source in range(1, RING):
        total = total + last[lax.rem(at_c - source + RING, RING)]
    spread_in[0] = (total * scale).astype(jnp.bfloat16)
    exchange(here, 1, lambda step: spread_in.at[0], spread_in, sends.at[3], recvs.at[3],
             lambda step: None)
    for source in range(rows // tile):
        chunk[0, source * tile : (source + 1) * tile] = spread_in[
            lax.rem(at_b - source + RING, RING)
        ]

    def across(step):
        return pltpu.make_async_remote_copy(
            src_ref=chunk.at[step], dst_ref=other_half.at[step],
            send_sem=pair_send.at[1 + step], recv_sem=pair_recv.at[1 + step],
            device_id=partner_of(here), device_id_type=MESH,
        )

    across(0).start()
    exchange(here, 0, lambda step: chunk.at[0], chunk, sends.at[4], recvs.at[4],
             lambda step: across(step).start())
    at_partner = at_a * 0 + here[2] * (1 - core) + here[1] * core

    def place(source, carry):
        out_ref[core, source] = chunk[lax.rem(at_a - source + RING, RING)]
        return carry

    lax.fori_loop(0, RING, place, 0)

    def settle(step, carry):
        across(step).wait()
        return carry

    lax.fori_loop(0, RING, settle, 0)

    def place_other(source, carry):
        out_ref[1 - core, source] = other_half[lax.rem(at_partner - source + RING, RING)]
        return carry

    lax.fori_loop(0, RING, place_other, 0)
    swap.wait_send()


def reduce_scratch(rows, lanes):
    tile = 16
    low, high = jnp.bfloat16, jnp.float32
    return [
        pltpu.VMEM((RING, rows, lanes), low),
        pltpu.VMEM((RING, rows, lanes), low),
        pltpu.VMEM((RING, rows, lanes), high),
        pltpu.VMEM((RING, rows, lanes), low),
        pltpu.VMEM((RING, rows, lanes), low),
        pltpu.VMEM((RING, tile, lanes), high),
        pltpu.VMEM((RING, tile, lanes), low),
        pltpu.VMEM((RING, tile, lanes), low),
        pltpu.VMEM((RING, tile, lanes), high),
        pltpu.VMEM((RING, tile, lanes), low),
        pltpu.VMEM((RING, rows, lanes), low),
        pltpu.VMEM((RING, rows, lanes), low),
        pltpu.VMEM((RING, rows, lanes), low),
        pltpu.SemaphoreType.DMA((1 + RING,)),
        pltpu.SemaphoreType.DMA((1 + RING,)),
        pltpu.SemaphoreType.DMA((5, RING)),
        pltpu.SemaphoreType.DMA((5, RING)),
    ]


def gelu_parts(pre):
    square = pre * pre
    bent = jnp.tanh(GELU_SLOPE * pre * (1.0 + GELU_CUBIC * square))
    value = 0.5 * pre * (1.0 + bent)
    slope = 0.5 * (1.0 + bent) + 0.5 * pre * (1.0 - bent * bent) * GELU_SLOPE * (
        1.0 + 3.0 * GELU_CUBIC * square
    )
    return value, slope


def halo_devices():
    lat = lax.axis_index("lat")
    lon = lax.axis_index("lon")
    lats = lax.axis_size("lat")
    lons = lax.axis_size("lon")
    at_top = lax.div(lats - 1 - lat, lats - 1)
    at_bottom = lax.div(lat, lats - 1)
    right = lax.rem(lon + 1, lons)
    left = lax.rem(lon + lons - 1, lons)
    ends = []
    for at_end, step, row_slot in ((at_top, -1, 1 - at_top), (at_bottom, 1, at_bottom)):
        far_lat = lat + step * (1 - at_end)
        turn = at_end * (lons // 2)
        ends.append(
            (
                row_slot,
                (far_lat, lax.rem(lon + turn, lons)),
                (far_lat, lax.rem(right + turn, lons)),
                (far_lat, lax.rem(left + turn, lons)),
            )
        )
    return (lat, right), (lat, left), ends


def greet_halo(barrier):
    right, left, ends = halo_devices()
    others = [right, left]
    for _, straight, to_right, to_left in ends:
        others += [straight, to_right, to_left]
    for other in others:
        pl.semaphore_signal(barrier, inc=1, device_id=other, device_id_type=MESH)
    return len(others)


def halo_outgoing(stage, halo):
    own, first_cols, last_cols, west, east, row_in, send_sem, recv_sem = halo
    rows = own.shape[1]
    right, left, ends = halo_devices()
    count = 0

    def copy(source, target, slot, device):
        nonlocal count
        count += 1
        return pltpu.make_async_remote_copy(
            src_ref=source, dst_ref=target, send_sem=send_sem.at[stage, count - 1],
            recv_sem=recv_sem.at[stage, slot], device_id=device, device_id_type=MESH,
        )

    outgoing = []
    for (slot, straight, to_right, to_left), row in zip(ends, (0, rows - 1)):
        edge = slot * (rows + 1)
        outgoing += [
            copy(last_cols.at[stage, row], west.at[stage, edge], 4 + slot, to_right),
            copy(first_cols.at[stage, row], east.at[stage, edge], 6 + slot, to_left),
            copy(own.at[stage, row], row_in.at[stage, slot], 2 + slot, straight),
        ]
    inner = pl.ds(1, rows)
    outgoing += [
        copy(last_cols.at[stage], west.at[stage, inner], 0, right),
        copy(first_cols.at[stage], east.at[stage, inner], 1, left),
    ]
    return outgoing


def halo_incoming(stage, halo):
    own, first_cols, last_cols, west, east, row_in, send_sem, recv_sem = halo
    rows = own.shape[1]
    right, left, _ = halo_devices()

    def copy(source, target, slot, device):
        return pltpu.make_async_remote_copy(
            src_ref=source, dst_ref=target, send_sem=send_sem.at[stage, slot],
            recv_sem=recv_sem.at[stage, slot], device_id=device, device_id_type=MESH,
        )

    inner = pl.ds(1, rows)
    incoming = [
        copy(last_cols.at[stage], west.at[stage, inner], 0, right),
        copy(first_cols.at[stage], east.at[stage, inner], 1, left),
    ]
    for slot in range(2):
        edge = slot * (rows + 1)
        incoming += [
            copy(own.at[stage, 0], row_in.at[stage, slot], 2 + slot, right),
            copy(last_cols.at[stage, 0], west.at[stage, edge], 4 + slot, right),
            copy(first_cols.at[stage, 0], east.at[stage, edge], 6 + slot, right),
        ]
    return incoming


def halo_prepare(stage, field, halo):
    own, first_cols, last_cols = halo[:3]
    own[stage] = field.astype(own.dtype)
    first_cols[stage] = field[:, :RIM].astype(own.dtype)
    last_cols[stage] = field[:, -RIM:].astype(own.dtype)


def halo_send(stage, halo):
    for copy in halo_outgoing(stage, halo):
        copy.start()


def halo_receive(stage, halo, extended):
    own, _, _, west, east, row_in = halo[:6]
    rows, cols = own.shape[1], own.shape[2]
    period = cols + 2 * RIM

    for row in range(rows):
        start = (row + 1) * period + 2 * RIM
        extended[start : start + cols] = own[stage, row]
    for copy in halo_incoming(stage, halo):
        copy.wait_recv()
    for slot in range(2):
        start = slot * (rows + 1) * period + 2 * RIM
        extended[start : start + cols] = row_in[stage, slot]
    west_rim = west[stage].astype(jnp.float32)
    east_rim = east[stage].astype(jnp.float32)
    blank = jnp.zeros((1, RIM, LANES), jnp.float32)
    rims = jnp.concatenate(
        [
            jnp.concatenate([blank, east_rim], axis=0),
            jnp.concatenate([west_rim, blank], axis=0),
        ],
        axis=1,
    ).astype(own.dtype)
    for row in range(rows + 3):
        extended[row * period : row * period + 2 * RIM] = rims[row]


def apply_bands(bands, extended, spread):
    rows, height = bands.shape[0], bands.shape[1]
    kernels = spread.shape[1] // LANES
    cols = spread.shape[0] // rows
    period = cols + 2 * RIM
    group = 4

    def some_rows(index, carry):
        for part in range(group):
            row = index * group + part
            window = extended[pl.ds(pl.multiple_of(row * period, period), LANES)]
            made = jnp.dot(
                bands[row], window, preferred_element_type=jnp.float32
            ).astype(spread.dtype)
            for kernel in range(kernels):
                spread[
                    pl.ds(pl.multiple_of(row * cols, cols), cols),
                    kernel * LANES : (kernel + 1) * LANES,
                ] = made[kernel * cols : (kernel + 1) * cols]
        return carry

    lax.fori_loop(0, rows // group, some_rows, 0)


def fill_bands(taps, bands, cols):
    rows, kernels = taps.shape[0], taps.shape[1]

    def one_row(row, carry):
        level = jnp.broadcast_to(taps[row][:, None, :], (kernels, cols, LANES))
        slanted = pltpu.roll(level, 0, 2, stride=1, stride_axis=1)
        bands[row] = slanted.reshape(kernels * cols, LANES).astype(bands.dtype)
        return carry

    lax.fori_loop(0, rows, one_row, 0)


def mixed_back(spread, weight):
    total = None
    for kernel in range(weight.shape[0]):
        term = lax.dot_general(
            spread[:, kernel * LANES : (kernel + 1) * LANES],
            weight[kernel],
            (((1,), (1,)), ((), ())),
            preferred_element_type=jnp.float32,
        )
        total = term if total is None else total + term
    return total


def whole_kernel(
    scale, fields, cotangent, weight_one, weight_two, taps_ahead, taps_back,
    output, dfields, grads,
    bands_ahead, bands_back, extended, u_one, u_two, v_vals, slope_one, dhidden, terms,
    own, first_cols, last_cols, west, east, row_in, halo_send_sem, halo_recv_sem, *scratch
):
    rows, cols, channels = fields.shape
    flat = (rows * cols, channels)
    halo = (own, first_cols, last_cols, west, east, row_in, halo_send_sem, halo_recv_sem)
    here = coordinates()
    barrier = pltpu.get_barrier_semaphore()
    awaited = greet_halo(barrier) + greet_reducers(here, barrier)

    halo_prepare(0, fields[...].astype(jnp.float32), halo)
    extended[...] = jnp.zeros(extended.shape, extended.dtype)
    fill_bands(taps_ahead, bands_ahead, cols)
    pl.semaphore_wait(barrier, awaited)
    halo_send(0, halo)
    fill_bands(taps_back, bands_back, cols)
    halo_receive(0, halo, extended)

    apply_bands(bands_ahead, extended, u_one)
    mix_one = weight_one[...].reshape(-1, channels)
    pre = jnp.dot(u_one[...], mix_one, preferred_element_type=jnp.float32)
    value, slope = gelu_parts(pre)
    slope_one[...] = slope
    hidden = fields[...].astype(jnp.float32) + value.reshape(rows, cols, channels)
    halo_prepare(1, hidden, halo)
    halo_send(1, halo)
    halo_receive(1, halo, extended)

    apply_bands(bands_ahead, extended, u_two)
    mix_two = weight_two[...].reshape(-1, channels)
    pre = jnp.dot(u_two[...], mix_two, preferred_element_type=jnp.float32)
    value, slope = gelu_parts(pre)
    upstream = cotangent[...].astype(jnp.float32)
    dconv = upstream * slope.reshape(rows, cols, channels)
    halo_prepare(2, dconv, halo)
    halo_send(2, halo)
    output[...] = (
        own[1].astype(jnp.float32) + value.reshape(rows, cols, channels)
    ).astype(output.dtype)
    terms[1] = lax.dot_general(
        u_two[...], own[2].reshape(flat), (((0,), (0,)), ((), ())),
        preferred_element_type=jnp.float32,
    ).reshape(terms.shape[1:])
    halo_receive(2, halo, extended)

    apply_bands(bands_back, extended, v_vals)
    arrived = upstream.reshape(flat) + mixed_back(v_vals, weight_two)
    dhidden[...] = arrived
    halo_prepare(3, (arrived * slope_one[...]).reshape(rows, cols, channels), halo)
    halo_send(3, halo)
    terms[0] = lax.dot_general(
        u_one[...], own[3].reshape(flat), (((0,), (0,)), ((), ())),
        preferred_element_type=jnp.float32,
    ).reshape(terms.shape[1:])

    def last_gradient():
        halo_receive(3, halo, extended)
        apply_bands(bands_back, extended, v_vals)
        total = dhidden[...] + mixed_back(v_vals, weight_one)
        dfields[...] = total.reshape(rows, cols, channels).astype(dfields.dtype)

    reduce_everywhere(here, terms, grads, scale, scratch, last_gradient)
    for stage in range(own.shape[0]):
        for copy in halo_outgoing(stage, halo):
            copy.wait_send()


def tap_lanes(taps):
    kernels, rows, row_taps, lon_taps = taps.shape
    lead = RIM + lon_taps // 2
    period = 4 * RIM
    spaced = jnp.pad(
        taps.transpose(1, 0, 2, 3).astype(jnp.float32),
        ((0, 0), (0, RING - kernels), (0, 0), (0, period - lon_taps)),
    ).reshape(rows, RING, row_taps * period)
    return jnp.pad(spaced, ((0, 0), (0, 0), (lead, LANES - lead - row_taps * period)))


def body(fields, weight_one, weight_two, basis_raw, widths, cotangent):
    rows, cols, channels = fields.shape
    kernels = weight_one.shape[0]
    basis = padded_basis(basis_raw, widths)
    first_row = lax.axis_index("lat") * rows
    ahead = lax.dynamic_slice_in_dim(basis, first_row + 2, rows, 1)
    around = lax.dynamic_slice_in_dim(basis, first_row + 1, rows + 2, 1)
    back = jnp.stack(
        [around[:, side : side + rows, 2 - side, ::-1] for side in range(3)], axis=2
    )
    scale = 1.0 / math.sqrt(rows * lax.axis_size("lat") * cols * lax.axis_size("lon"))
    grad_rows = kernels * channels // RING
    low, high = jnp.bfloat16, jnp.float32
    height = (rows + 3) * (cols + 2 * RIM)
    stages = 4
    scratch = [
        pltpu.VMEM((rows, RING * cols, LANES), low),
        pltpu.VMEM((rows, RING * cols, LANES), low),
        pltpu.VMEM((height, channels), low),
        pltpu.VMEM((rows * cols, kernels * channels), low),
        pltpu.VMEM((rows * cols, kernels * channels), low),
        pltpu.VMEM((rows * cols, kernels * channels), low),
        pltpu.VMEM((rows * cols, channels), high),
        pltpu.VMEM((rows * cols, channels), high),
        pltpu.VMEM((2, RING, grad_rows, channels), high),
        pltpu.VMEM((stages, rows, cols, channels), low),
        pltpu.VMEM((stages, rows, RIM, channels), low),
        pltpu.VMEM((stages, rows, RIM, channels), low),
        pltpu.VMEM((stages, rows + 2, RIM, channels), low),
        pltpu.VMEM((stages, rows + 2, RIM, channels), low),
        pltpu.VMEM((stages, 2, cols, channels), low),
        pltpu.SemaphoreType.DMA((stages, 8)),
        pltpu.SemaphoreType.DMA((stages, 8)),
    ] + reduce_scratch(grad_rows, channels)
    output, dfields, grads = pl.pallas_call(
        functools.partial(whole_kernel, scale),
        out_shape=(
            jax.ShapeDtypeStruct(fields.shape, low),
            jax.ShapeDtypeStruct(fields.shape, low),
            jax.ShapeDtypeStruct((2, RING, grad_rows, channels), low),
        ),
        in_specs=[pl.BlockSpec(memory_space=pltpu.VMEM)] * 6,
        out_specs=(pl.BlockSpec(memory_space=pltpu.VMEM),) * 3,
        scratch_shapes=scratch,
        compiler_params=pltpu.CompilerParams(collective_id=0, has_side_effects=True),
    )(fields, cotangent, weight_one, weight_two, tap_lanes(ahead), tap_lanes(back))
    grads = grads.astype(jnp.float32).reshape(2, kernels, channels, channels)
    return output, dfields, grads[0], grads[1]


def solution(mesh):
    placed = (P("lat", "lon", None), P(), P(), P(), P(), P("lat", "lon", None))
    return jax.shard_map(
        body,
        mesh=mesh,
        in_specs=placed,
        out_specs=(P("lat", "lon", None), P("lat", "lon", None), P(), P()),
        check_vma=False,
    )
```

time: 159 us -> 80.4 us (0.51); the launches traced: 157 us -> 80.1 us
  starting transfers between devices: 88.6 us -> 0 us
  Pallas kernels: 37.4 us -> 72.6 us
  matrix products: 10.6 us -> 0 us
  waiting for transfers between devices: 10.5 us -> 0 us
    ppermute x20 -> x0, starting transfers between devices: 88.6 us -> none  [the longest x8 50.9 us: with_halo(): lax.ppermute(lax.slice_in_dim(block, 0, width, axis=dim), axis, backward)]
    pallas_call x1, Pallas kernels: 37.4 us -> 72.6 us  [body(): pl.pallas_call(functools.partial(whole_kernel, scale), out_shape=(jax.Sha...]
    dot_general x24 -> x0, matrix products: 10.6 us -> none  [the longest x6 3.6 us: gather_back(): jnp.einsum('kjlm,jmkc->jlc', band_rows, extended[first_tap:first_tap + ro...]
    ppermute x20 -> x0, waiting for transfers between devices: 10.5 us -> none  [the longest x4 4.64 us: shifted(): return lax.ppermute(block, axis, route)]
  transfers between devices with their start and end apart: 20 -> 0, of which waited for: 8 -> 0; matrix products, arithmetic and copies ran while one was open for 6% -> 0% of each run, Pallas kernels for 24% -> 0%
where the time goes in v2:
time: 80.4 us; the launch traced here: 80.1 us
  Pallas kernels  72.6 us (90%)
  local copies, waits for them, and re-layouts  5.05 us (6%)
  other arithmetic  1.67 us (2%)
    pallas_call x1, Pallas kernels, body(): pl.pallas_call(functools.partial(whole_kernel, scale), out_shape=(jax.Sha...  72.6 us
    unnamed x8, local copies, waits for them, and re-layouts  2.13 us
    slice x1, local copies, waits for them, and re-layouts, body(): return (output, dfields, grads[0], grads[1])  2.06 us

profile of v2, /device:TPU:1, one launch (start us, length us, event | category | flops | bytes accessed | tf_op | source)
XLA Modules:
  0.0 80.1 jit_solution(927118741235196723)
XLA Ops:
  0.6 0.0 copy-start.2
  0.7 0.6 copy-done.2
  1.3 0.1 compare_convert_fusion
  1.4 0.8 %broadcast_multiply_fusion = bf16[7,64,3,9]{1,0,3,2:T(8,128)(2,1)S(1)} fusion(bf16[7,64,3,9]{1,0,3,2:T(8,128)(2,1)} %param.9, bf16[64,9]{0,1:T(8,128)(2,1)S(1)} %compare_convert_fusion), kind=kLoop, calls=%fused_computation.4 | loop fusion | flops 12096 | bytes 49536 | tf_op jit(solution)/shard_map/mul | solution.py:24
  2.2 0.1 fusion.1
  2.3 0.2 concatenate.3
  2.5 0.1 constant_dynamic-slice_fusion.1
  2.6 0.1 dynamic-slice_bitcast_fusion
  2.8 0.2 copy.15
  3.0 0.2 copy.14
  3.2 0.7 pad_convert_fusion
  3.9 72.6 %shard_map.93 = (bf16[16,16,128]{2,1,0:T(8,128)(2,1)}, bf16[16,16,128]{2,1,0:T(8,128)(2,1)}, bf16[2,8,112,128]{3,2,1,0:T(8,128)(2,1)}) custom-call(bf16[16,16,128]{2,1,0:T(8,128)(2,1)} %fields.1, bf16[16,16,128]{2,1,0:T(8,128)(2,1)} %cotangent.1, bf16[7,128,128]{2,1,0:T(8,128)(2,1)} %weight_one.1, bf16[7,128,128]{2,1,0:T(8,128)(2,1)} %weight_two.1, ...), custom_call_target="tpu_custom_call" | custom-call | tf_op jit(solution)/shard_map/pallas_call | solution.py:519
  76.5 0.0 copy-start.1
  76.5 2.1 %fusion = (f32[1,8,112,128]{3,2,1,0:T(8,128)}, f32[1,8,112,128]{3,2,1,0:T(8,128)}) fusion(bf16[2,8,112,128]{3,2,1,0:T(8,128)(2,1)} %get-tuple-element.9), kind=kLoop, calls=%fused_computation.10 | loop fusion | bytes 1835008 | tf_op jit(solution)/shard_map/slice | solution.py:532
  78.6 0.0 copy-done.1
  78.6 0.0 copy-start
  78.6 0.6 copy.18
  79.2 0.2 copy-done
  79.4 0.6 copy.19
  (10 shorter events, 0.1 us)
Async XLA Ops:
  0.6 0.7 copy-start.2
  76.5 2.1 %copy-start.1 = (bf16[16,16,128]{2,1,0:T(8,128)(2,1)S(1)}, bf16[16,16,128]{2,1,0:T(8,128)(2,1)}, u32[]{:S(2)}) copy-start(bf16[16,16,128]{2,1,0:T(8,128)(2,1)} %get-tuple-element.23) | copy-start | bytes 196612
  78.6 0.9 %copy-start = (bf16[16,16,128]{2,1,0:T(8,128)(2,1)S(1)}, bf16[16,16,128]{2,1,0:T(8,128)(2,1)}, u32[]{:S(2)}) copy-start(bf16[16,16,128]{2,1,0:T(8,128)(2,1)} %get-tuple-element.24) | copy-start | bytes 196612

commit v3 on v2

--- a/solution.py
+++ b/solution.py
@@ -79,137 +79,137 @@
     return 1 + 3 * (RING - 1)
 
 
-def exchange(here, stage, source_of, landing, send_sem, recv_sem, arrived, meanwhile=None):
-    def copy(step):
+FAR_FIRST = (4, 3, 5, 2, 6, 1, 7)
+NEAR_FIRST = (1, 7, 2, 6, 3, 5, 4)
+
+
+class Chain:
+    def __init__(self, which, here, terms, result, scale, scratch):
+        (self.pair_out, self.pair_in, self.halves, self.wide_out, self.wide_in, self.middle,
+         self.last, self.chunk, self.other_half) = (ref.at[which] for ref in scratch[:9])
+        self.pair_send, self.pair_recv, self.sends, self.recvs = (
+            ref.at[which] for ref in scratch[9:]
+        )
+        self.here, self.terms, self.result, self.scale = here, terms.at[which], result, scale
+        self.core = here[0]
+        self.at = [ring_index(here, axis) for axis in range(3)]
+
+    def pair_copy(self, source, target, slot):
         return pltpu.make_async_remote_copy(
-            src_ref=source_of(step),
-            dst_ref=landing.at[step],
-            send_sem=send_sem.at[step],
-            recv_sem=recv_sem.at[step],
-            device_id=ring_peer(here, stage, step),
+            src_ref=source, dst_ref=target, send_sem=self.pair_send.at[slot],
+            recv_sem=self.pair_recv.at[slot], device_id=partner_of(self.here),
             device_id_type=MESH,
         )
 
-    def start(step, carry):
-        copy(step).start()
-        return carry
-
-    def finish(step, carry):
-        copy(step).wait_recv()
-        arrived(step)
-        return carry
-
-    def drain(step, carry):
-        copy(step).wait_send()
-        return carry
-
-    lax.fori_loop(1, RING, start, 0)
-    if meanwhile is not None:
-        meanwhile()
-    lax.fori_loop(1, RING, finish, 0)
-    lax.fori_loop(1, RING, drain, 0)
-
-
-def reduce_everywhere(here, terms, out_ref, scale, scratch, meanwhile):
-    (pair_out, pair_in, halves, wide_out, wide_in, narrow, narrow_out, narrow_in,
-     last, spread_in, chunk, own_half, other_half, pair_send, pair_recv, sends, recvs) = scratch
-    core = here[0]
-    pair_out[...] = terms[1 - core].astype(jnp.bfloat16)
-    swap = pltpu.make_async_remote_copy(
-        src_ref=pair_out, dst_ref=pair_in, send_sem=pair_send.at[0], recv_sem=pair_recv.at[0],
-        device_id=partner_of(here), device_id_type=MESH,
-    )
-    swap.start()
-    narrow[...] = jnp.zeros(narrow.shape, narrow.dtype)
-    swap.wait_recv()
-    halves[...] = terms[core] + pair_in[...].astype(jnp.float32)
-    wide_out[...] = halves[...].astype(jnp.bfloat16)
-
-    at_a, at_b, at_c = (ring_index(here, stage) for stage in range(3))
-    rows = halves.shape[1]
-    tile = narrow.shape[1]
-    own = narrow.at[: rows // tile]
-    own[...] = halves[at_a].reshape(rows // tile, tile, -1)
-
-    def add_wide(step):
-        own[...] += wide_in[step].astype(jnp.float32).reshape(rows // tile, tile, -1)
-
-    exchange(here, 0, lambda step: wide_out.at[lax.rem(at_a + step, RING)], wide_in,
-             sends.at[0], recvs.at[0], add_wide, meanwhile)
-    narrow_out[...] = narrow[...].astype(jnp.bfloat16)
-    last[0] = narrow[at_b]
-
-    def add_narrow(step):
-        last[0] += narrow_in[step].astype(jnp.float32)
-
-    exchange(here, 1, lambda step: narrow_out.at[lax.rem(at_b + step, RING)], narrow_in,
-             sends.at[1], recvs.at[1], add_narrow)
-    exchange(here, 2, lambda step: last.at[0], last, sends.at[2], recvs.at[2], lambda step: None)
-
-    total = last[at_c]
-    for source in range(1, RING):
-        total = total + last[lax.rem(at_c - source + RING, RING)]
-    spread_in[0] = (total * scale).astype(jnp.bfloat16)
-    exchange(here, 1, lambda step: spread_in.at[0], spread_in, sends.at[3], recvs.at[3],
-             lambda step: None)
-    for source in range(rows // tile):
-        chunk[0, source * tile : (source + 1) * tile] = spread_in[
-            lax.rem(at_b - source + RING, RING)
-        ]
-
-    def across(step):
+    def swap(self):
+        return self.pair_copy(self.pair_out, self.pair_in, RING)
+
+    def across(self, step):
+        return self.pair_copy(self.chunk.at[step], self.other_half.at[step], step)
+
+    def ring_copy(self, stage, axis, source, landing, step):
         return pltpu.make_async_remote_copy(
-            src_ref=chunk.at[step], dst_ref=other_half.at[step],
-            send_sem=pair_send.at[1 + step], recv_sem=pair_recv.at[1 + step],
-            device_id=partner_of(here), device_id_type=MESH,
-        )
-
-    across(0).start()
-    exchange(here, 0, lambda step: chunk.at[0], chunk, sends.at[4], recvs.at[4],
-             lambda step: across(step).start())
-    at_partner = at_a * 0 + here[2] * (1 - core) + here[1] * core
-
-    def place(source, carry):
-        out_ref[core, source] = chunk[lax.rem(at_a - source + RING, RING)]
-        return carry
-
-    lax.fori_loop(0, RING, place, 0)
-
-    def settle(step, carry):
-        across(step).wait()
-        return carry
-
-    lax.fori_loop(0, RING, settle, 0)
-
-    def place_other(source, carry):
-        out_ref[1 - core, source] = other_half[lax.rem(at_partner - source + RING, RING)]
-        return carry
-
-    lax.fori_loop(0, RING, place_other, 0)
-    swap.wait_send()
+            src_ref=source, dst_ref=landing.at[step], send_sem=self.sends.at[stage, step],
+            recv_sem=self.recvs.at[stage, step],
+            device_id=ring_peer(self.here, axis, step), device_id_type=MESH,
+        )
+
+    def wide_copy(self, step):
+        source = self.wide_out.at[lax.rem(self.at[0] + step, RING)]
+        return self.ring_copy(0, 0, source, self.wide_in, step)
+
+    def middle_copy(self, step):
+        return self.ring_copy(1, 1, self.middle.at[0], self.middle, step)
+
+    def last_copy(self, step):
+        return self.ring_copy(2, 2, self.last.at[0], self.last, step)
+
+    def chunk_copy(self, step):
+        return self.ring_copy(3, 0, self.chunk.at[0], self.chunk, step)
+
+    def begin(self):
+        self.pair_out[...] = self.terms[1 - self.core].astype(jnp.bfloat16)
+        self.swap().start()
+
+    def scatter(self):
+        self.swap().wait_recv()
+        both = self.terms[self.core] + self.pair_in[...].astype(jnp.float32)
+        self.halves[...] = both
+        self.wide_out[...] = both.astype(jnp.bfloat16)
+        for step in FAR_FIRST:
+            self.wide_copy(step).start()
+
+    def sum_first(self):
+        total = self.halves[self.at[0]]
+        for step in NEAR_FIRST:
+            self.wide_copy(step).wait_recv()
+            total = total + self.wide_in[step].astype(jnp.float32)
+        self.middle[0] = total.astype(jnp.bfloat16)
+        for step in FAR_FIRST:
+            self.middle_copy(step).start()
+
+    def in_order(self, landing, axis):
+        total = None
+        for source in range(RING):
+            term = landing[lax.rem(self.at[axis] - source + RING, RING)].astype(jnp.float32)
+            total = term if total is None else total + term
+        return total
+
+    def sum_second(self):
+        for step in NEAR_FIRST:
+            self.middle_copy(step).wait_recv()
+        self.last[0] = self.in_order(self.middle, 1).astype(jnp.bfloat16)
+        for step in FAR_FIRST:
+            self.last_copy(step).start()
+
+    def sum_third(self):
+        for step in NEAR_FIRST:
+            self.last_copy(step).wait_recv()
+        self.chunk[0] = (self.in_order(self.last, 2) * self.scale).astype(jnp.bfloat16)
+        for step in FAR_FIRST:
+            self.chunk_copy(step).start()
+        self.across(0).start()
+
+    def gather(self):
+        core, x, y, _ = self.here
+        for step in NEAR_FIRST:
+            self.chunk_copy(step).wait_recv()
+            self.across(step).start()
+        for source in range(RING):
+            self.result[core, source] = self.chunk[
+                lax.rem(self.at[0] - source + RING, RING)
+            ].astype(jnp.float32)
+        at_partner = y * (1 - core) + x * core
+        for step in (0,) + NEAR_FIRST:
+            self.across(step).wait_recv()
+        for source in range(RING):
+            self.result[1 - core, source] = self.other_half[
+                lax.rem(at_partner - source + RING, RING)
+            ].astype(jnp.float32)
+
+    def drain(self):
+        self.swap().wait_send()
+        for step in range(RING):
+            self.across(step).wait_send()
+
+        def one(step, carry):
+            self.wide_copy(step).wait_send()
+            self.middle_copy(step).wait_send()
+            self.last_copy(step).wait_send()
+            self.chunk_copy(step).wait_send()
+            return carry
+
+        lax.fori_loop(1, RING, one, 0)
 
 
 def reduce_scratch(rows, lanes):
-    tile = 16
     low, high = jnp.bfloat16, jnp.float32
-    return [
-        pltpu.VMEM((RING, rows, lanes), low),
-        pltpu.VMEM((RING, rows, lanes), low),
-        pltpu.VMEM((RING, rows, lanes), high),
-        pltpu.VMEM((RING, rows, lanes), low),
-        pltpu.VMEM((RING, rows, lanes), low),
-        pltpu.VMEM((RING, tile, lanes), high),
-        pltpu.VMEM((RING, tile, lanes), low),
-        pltpu.VMEM((RING, tile, lanes), low),
-        pltpu.VMEM((RING, tile, lanes), high),
-        pltpu.VMEM((RING, tile, lanes), low),
-        pltpu.VMEM((RING, rows, lanes), low),
-        pltpu.VMEM((RING, rows, lanes), low),
-        pltpu.VMEM((RING, rows, lanes), low),
-        pltpu.SemaphoreType.DMA((1 + RING,)),
-        pltpu.SemaphoreType.DMA((1 + RING,)),
-        pltpu.SemaphoreType.DMA((5, RING)),
-        pltpu.SemaphoreType.DMA((5, RING)),
+    kinds = [low, low, high, low, low, low, low, low, low]
+    return [pltpu.VMEM((2, RING, rows, lanes), kind) for kind in kinds] + [
+        pltpu.SemaphoreType.DMA((2, 1 + RING)),
+        pltpu.SemaphoreType.DMA((2, 1 + RING)),
+        pltpu.SemaphoreType.DMA((2, 4, RING)),
+        pltpu.SemaphoreType.DMA((2, 4, RING)),
     ]
 
 
@@ -403,7 +403,7 @@
 
 def whole_kernel(
     scale, fields, cotangent, weight_one, weight_two, taps_ahead, taps_back,
-    output, dfields, grads,
+    output, dfields, grad_one, grad_two,
     bands_ahead, bands_back, extended, u_one, u_two, v_vals, slope_one, dhidden, terms,
     own, first_cols, last_cols, west, east, row_in, halo_send_sem, halo_recv_sem, *scratch
 ):
@@ -411,6 +411,8 @@
     flat = (rows * cols, channels)
     halo = (own, first_cols, last_cols, west, east, row_in, halo_send_sem, halo_recv_sem)
     here = coordinates()
+    chain_one = Chain(0, here, terms, grad_one, scale, scratch)
+    chain_two = Chain(1, here, terms, grad_two, scale, scratch)
     barrier = pltpu.get_barrier_semaphore()
     awaited = greet_halo(barrier) + greet_reducers(here, barrier)
 
@@ -447,25 +449,39 @@
         u_two[...], own[2].reshape(flat), (((0,), (0,)), ((), ())),
         preferred_element_type=jnp.float32,
     ).reshape(terms.shape[1:])
+    chain_two.begin()
     halo_receive(2, halo, extended)
+    chain_two.scatter()
 
     apply_bands(bands_back, extended, v_vals)
     arrived = upstream.reshape(flat) + mixed_back(v_vals, weight_two)
     dhidden[...] = arrived
-    halo_prepare(3, (arrived * slope_one[...]).reshape(rows, cols, channels), halo)
-    halo_send(3, halo)
+    dconv = (arrived * slope_one[...]).reshape(rows, cols, channels)
+    own[3] = dconv.astype(own.dtype)
     terms[0] = lax.dot_general(
         u_one[...], own[3].reshape(flat), (((0,), (0,)), ((), ())),
         preferred_element_type=jnp.float32,
     ).reshape(terms.shape[1:])
-
-    def last_gradient():
-        halo_receive(3, halo, extended)
-        apply_bands(bands_back, extended, v_vals)
-        total = dhidden[...] + mixed_back(v_vals, weight_one)
-        dfields[...] = total.reshape(rows, cols, channels).astype(dfields.dtype)
-
-    reduce_everywhere(here, terms, grads, scale, scratch, last_gradient)
+    chain_one.begin()
+    halo_prepare(3, dconv, halo)
+    halo_send(3, halo)
+    chain_two.sum_first()
+    chain_one.scatter()
+    chain_two.sum_second()
+
+    halo_receive(3, halo, extended)
+    apply_bands(bands_back, extended, v_vals)
+    total = dhidden[...] + mixed_back(v_vals, weight_one)
+    dfields[...] = total.reshape(rows, cols, channels).astype(dfields.dtype)
+
+    chain_one.sum_first()
+    chain_two.sum_third()
+    chain_one.sum_second()
+    chain_two.gather()
+    chain_one.sum_third()
+    chain_two.drain()
+    chain_one.gather()
+    chain_one.drain()
     for stage in range(own.shape[0]):
         for copy in halo_outgoing(stage, halo):
             copy.wait_send()
@@ -493,7 +509,7 @@
         [around[:, side : side + rows, 2 - side, ::-1] for side in range(3)], axis=2
     )
     scale = 1.0 / math.sqrt(rows * lax.axis_size("lat") * cols * lax.axis_size("lon"))
-    grad_rows = kernels * channels // RING
+    grad_rows = kernels * channels // (2 * RING)
     low, high = jnp.bfloat16, jnp.float32
     height = (rows + 3) * (cols + 2 * RIM)
     stages = 4
@@ -506,7 +522,7 @@
         pltpu.VMEM((rows * cols, kernels * channels), low),
         pltpu.VMEM((rows * cols, channels), high),
         pltpu.VMEM((rows * cols, channels), high),
-        pltpu.VMEM((2, RING, grad_rows, channels), high),
+        pltpu.VMEM((2, 2, RING, grad_rows, channels), high),
         pltpu.VMEM((stages, rows, cols, channels), low),
         pltpu.VMEM((stages, rows, RIM, channels), low),
         pltpu.VMEM((stages, rows, RIM, channels), low),
@@ -516,20 +532,22 @@
         pltpu.SemaphoreType.DMA((stages, 8)),
         pltpu.SemaphoreType.DMA((stages, 8)),
     ] + reduce_scratch(grad_rows, channels)
-    output, dfields, grads = pl.pallas_call(
+    wide = jax.ShapeDtypeStruct((2, RING, grad_rows, channels), high)
+    output, dfields, grad_one, grad_two = pl.pallas_call(
         functools.partial(whole_kernel, scale),
         out_shape=(
             jax.ShapeDtypeStruct(fields.shape, low),
             jax.ShapeDtypeStruct(fields.shape, low),
-            jax.ShapeDtypeStruct((2, RING, grad_rows, channels), low),
+            wide,
+            wide,
         ),
         in_specs=[pl.BlockSpec(memory_space=pltpu.VMEM)] * 6,
-        out_specs=(pl.BlockSpec(memory_space=pltpu.VMEM),) * 3,
+        out_specs=(pl.BlockSpec(memory_space=pltpu.VMEM),) * 4,
         scratch_shapes=scratch,
         compiler_params=pltpu.CompilerParams(collective_id=0, has_side_effects=True),
     )(fields, cotangent, weight_one, weight_two, tap_lanes(ahead), tap_lanes(back))
-    grads = grads.astype(jnp.float32).reshape(2, kernels, channels, channels)
-    return output, dfields, grads[0], grads[1]
+    shape = (kernels, channels, channels)
+    return output, dfields, grad_one.reshape(shape), grad_two.reshape(shape)
 
 
 def solution(mesh):

time: 80.4 us -> 79.4 us (0.988)
  Pallas kernels: 72.6 us -> 70.4 us
  local copies, waits for them, and re-layouts: 5.05 us -> 6.27 us
    unnamed x8 -> x10, local copies, waits for them, and re-layouts: 2.13 us -> 5.42 us
    pallas_call x1, Pallas kernels: 72.6 us -> 70.4 us  [body(): pl.pallas_call(functools.partial(whole_kernel, scale), out_shape=(jax.Sha...]
    slice x1 -> x0, local copies, waits for them, and re-layouts: 2.06 us -> none  [body(): return (output, dfields, grads[0], grads[1])]
where the time goes in v3:
time: 79.4 us; the launch traced here: 79.1 us
  Pallas kernels  70.4 us (89%)
  local copies, waits for them, and re-layouts  6.27 us (8%)
  other arithmetic  1.67 us (2%)
    pallas_call x1, Pallas kernels, body(): pl.pallas_call(functools.partial(whole_kernel, scale), out_shape=(jax.Sha...  70.4 us
    unnamed x10, local copies, waits for them, and re-layouts  5.42 us

profile of v3, /device:TPU:1, one launch (start us, length us, event | category | flops | bytes accessed | tf_op | source)
XLA Modules:
  0.0 79.1 jit_solution(10304637129126073113)
XLA Ops:
  0.6 0.0 copy-start.2
  0.7 0.6 copy-done.2
  1.3 0.1 compare_convert_fusion
  1.4 0.8 %broadcast_multiply_fusion = bf16[7,64,3,9]{1,0,3,2:T(8,128)(2,1)S(1)} fusion(bf16[7,64,3,9]{1,0,3,2:T(8,128)(2,1)} %param.9, bf16[64,9]{0,1:T(8,128)(2,1)S(1)} %compare_convert_fusion), kind=kLoop, calls=%fused_computation.4 | loop fusion | flops 12096 | bytes 49536 | tf_op jit(solution)/shard_map/mul | solution.py:24
  2.2 0.1 fusion
  2.3 0.2 concatenate.3
  2.5 0.1 constant_dynamic-slice_fusion.1
  2.6 0.1 dynamic-slice_bitcast_fusion
  2.8 0.2 copy.15
  3.0 0.2 copy.14
  3.2 0.7 pad_convert_fusion
  3.9 70.4 %shard_map.93 = (bf16[16,16,128]{2,1,0:T(8,128)(2,1)}, bf16[16,16,128]{2,1,0:T(8,128)(2,1)}, f32[2,8,56,128]{3,2,1,0:T(8,128)}, f32[2,8,56,128]{3,2,1,0:T(8,128)}) custom-call(bf16[16,16,128]{2,1,0:T(8,128)(2,1)} %fields.1, bf16[16,16,128]{2,1,0:T(8,128)(2,1)} %cotangent.1, bf16[7,128,128]{2,1,0:T(8,128)(2,1)} %weight_one.1, ...), custom_call_target="tpu_custom_call" | custom-call | tf_op jit(solution)/shard_map/pallas_call | solution.py:536
  74.3 0.0 copy-start.1
  74.3 1.5 %copy.20 = bf16[16,16,128]{2,1,0:T(8,128)(2,1)} copy(bf16[16,16,128]{2,1,0:T(8,128)(2,1)} %get-tuple-element.23) | data formatting | bytes 131072
  75.8 0.0 copy-done.1
  75.8 0.6 copy.21
  76.5 0.0 copy-start
  76.5 1.9 %copy.22 = f32[7,128,128]{2,1,0:T(8,128)} copy(f32[7,128,128]{2,1,0:T(8,128)} %bitcast.11) | data formatting | bytes 917504
  78.4 0.0 copy-done
  78.4 0.8 copy.23
  (10 shorter events, 0.1 us)
Async XLA Ops:
  0.6 0.7 copy-start.2
  74.3 1.5 %copy-start.1 = (bf16[16,16,128]{2,1,0:T(8,128)(2,1)S(1)}, bf16[16,16,128]{2,1,0:T(8,128)(2,1)}, u32[]{:S(2)}) copy-start(bf16[16,16,128]{2,1,0:T(8,128)(2,1)} %get-tuple-element.24) | copy-start | bytes 196612
  76.5 1.9 %copy-start = (f32[2,8,56,128]{3,2,1,0:T(8,128)S(1)}, f32[2,8,56,128]{3,2,1,0:T(8,128)}, u32[]{:S(2)}) copy-start(f32[2,8,56,128]{3,2,1,0:T(8,128)} %get-tuple-element.11) | copy-start | bytes 1376260

commit v4 on v3

--- a/solution.py
+++ b/solution.py
@@ -1,4 +1,3 @@
-import functools
 import math
 
 import jax
@@ -14,18 +13,6 @@
 LANES = 128
 GELU_SLOPE = math.sqrt(2.0 / math.pi)
 GELU_CUBIC = 0.044715
-
-
-def padded_basis(basis_raw, widths):
-    tap_count = basis_raw.shape[3]
-    reach = (tap_count - 1) // 2
-    distance = jnp.abs(jnp.arange(tap_count, dtype=jnp.int32) - reach)
-    inside = (distance[None, :] <= widths[:, None]).astype(jnp.bfloat16)
-    masked = basis_raw * inside[None, :, None, :]
-    top_rows = masked[:, 0:1, ::-1, :]
-    bottom = masked[:, -1:, ::-1, :]
-    zero_row = jnp.zeros_like(top_rows)
-    return jnp.concatenate([zero_row, top_rows, masked, bottom, zero_row], axis=1)
 
 
 def coordinates():
@@ -84,13 +71,13 @@
 
 
 class Chain:
-    def __init__(self, which, here, terms, result, scale, scratch):
+    def __init__(self, which, here, terms, result, scratch):
         (self.pair_out, self.pair_in, self.halves, self.wide_out, self.wide_in, self.middle,
          self.last, self.chunk, self.other_half) = (ref.at[which] for ref in scratch[:9])
         self.pair_send, self.pair_recv, self.sends, self.recvs = (
             ref.at[which] for ref in scratch[9:]
         )
-        self.here, self.terms, self.result, self.scale = here, terms.at[which], result, scale
+        self.here, self.terms, self.result = here, terms.at[which], result
         self.core = here[0]
         self.at = [ring_index(here, axis) for axis in range(3)]
 
@@ -165,7 +152,7 @@
     def sum_third(self):
         for step in NEAR_FIRST:
             self.last_copy(step).wait_recv()
-        self.chunk[0] = (self.in_order(self.last, 2) * self.scale).astype(jnp.bfloat16)
+        self.chunk[0] = self.in_order(self.last, 2).astype(jnp.bfloat16)
         for step in FAR_FIRST:
             self.chunk_copy(step).start()
         self.across(0).start()
@@ -353,7 +340,7 @@
 
 
 def apply_bands(bands, extended, spread):
-    rows, height = bands.shape[0], bands.shape[1]
+    rows = bands.shape[0]
     kernels = spread.shape[1] // LANES
     cols = spread.shape[0] // rows
     period = cols + 2 * RIM
@@ -376,13 +363,86 @@
     lax.fori_loop(0, rows // group, some_rows, 0)
 
 
-def fill_bands(taps, bands, cols):
-    rows, kernels = taps.shape[0], taps.shape[1]
+def load_taps(basis, taps, first, at_top, at_bottom):
+    kernels, _, row_taps, lon_taps = basis.shape
+    rows = taps.shape[1] - 2
+    low_end, high_end = row_taps - 1, 0
+    taps[...] = jnp.zeros(taps.shape, taps.dtype)
+
+    def one_kernel(kernel, carry):
+        taps[kernel, 1 : rows + 1, :row_taps, :lon_taps] = basis[
+            kernel, pl.ds(first, rows)
+        ].astype(taps.dtype)
+        above = basis[kernel, first - 1 + at_top].astype(taps.dtype)
+        below = basis[kernel, first + rows - at_bottom].astype(taps.dtype)
+        taps[kernel, 0, low_end : low_end + 1, :lon_taps] = jnp.where(
+            at_top == 1, above[:1], above[low_end:]
+        )
+        taps[kernel, rows + 1, high_end : high_end + 1, :lon_taps] = jnp.where(
+            at_bottom == 1, below[low_end:], below[:1]
+        )
+        return carry
+
+    lax.fori_loop(0, kernels, one_kernel, 0)
+
+
+def slant(lined, cols):
+    kernels = lined.shape[0]
+    level = jnp.broadcast_to(jnp.sum(lined, axis=1, keepdims=True), (kernels, cols, LANES))
+    return pltpu.roll(level, 0, 2, stride=1, stride_axis=1).reshape(kernels * cols, LANES)
+
+
+def fan_out(lined, start, stride):
+    sublane = lax.broadcasted_iota(jnp.int32, lined.shape, 1)
+    total = None
+    for row_tap in range(3):
+        moved = pltpu.roll(lined, (start + stride * row_tap) % LANES, 2)
+        moved = jnp.where(sublane == row_tap, moved, 0.0)
+        total = moved if total is None else total + moved
+    return total
+
+
+def within(shape, widths, row):
+    offset = lax.broadcasted_iota(jnp.int32, shape, 2) - RIM // 2
+    return jnp.abs(offset) <= widths[row]
+
+
+def fill_ahead(taps, widths, bands, first, cols):
+    rows = bands.shape[0]
+    lead = RIM + RIM // 2
 
     def one_row(row, carry):
-        level = jnp.broadcast_to(taps[row][:, None, :], (kernels, cols, LANES))
-        slanted = pltpu.roll(level, 0, 2, stride=1, stride_axis=1)
-        bands[row] = slanted.reshape(kernels * cols, LANES).astype(bands.dtype)
+        seen = taps[:, row + 1]
+        seen = jnp.where(within(seen.shape, widths, first + row), seen, 0.0)
+        lined = fan_out(seen, lead, 4 * RIM)
+        bands[row] = slant(lined, cols).astype(bands.dtype)
+        return carry
+
+    lax.fori_loop(0, rows, one_row, 0)
+
+
+def fill_back(taps, widths, bands, first, last_row, cols):
+    rows = bands.shape[0]
+    lead = RIM + RIM // 2 + 2 * 4 * RIM + RIM
+    kernels = taps.shape[0]
+    lane_from = lax.broadcasted_iota(jnp.int32, (LANES, LANES), 0)
+    lane_to = lax.broadcasted_iota(jnp.int32, (LANES, LANES), 1)
+    turned = jnp.where(lane_from + lane_to == lead, 1.0, 0.0).astype(jnp.bfloat16)
+
+    def one_row(row, carry):
+        picked = None
+        for row_tap in range(3):
+            source = taps[:, row + 2 - row_tap]
+            at = jnp.minimum(jnp.maximum(first + row + 1 - row_tap, 0), last_row)
+            sublane = lax.broadcasted_iota(jnp.int32, source.shape, 1)
+            kept = jnp.where(within(source.shape, widths, at) & (sublane == row_tap), source, 0.0)
+            picked = kept if picked is None else picked + kept
+        flipped = jnp.dot(
+            picked.reshape(kernels * RING, LANES).astype(jnp.bfloat16), turned,
+            preferred_element_type=jnp.float32,
+        ).reshape(picked.shape)
+        lined = fan_out(flipped, 0, LANES - 4 * RIM)
+        bands[row] = slant(lined, cols).astype(bands.dtype)
         return carry
 
     lax.fori_loop(0, rows, one_row, 0)
@@ -402,26 +462,30 @@
 
 
 def whole_kernel(
-    scale, fields, cotangent, weight_one, weight_two, taps_ahead, taps_back,
+    fields, cotangent, weight_one, weight_two, basis, widths,
     output, dfields, grad_one, grad_two,
-    bands_ahead, bands_back, extended, u_one, u_two, v_vals, slope_one, dhidden, terms,
+    taps, bands_ahead, bands_back, extended, u_one, u_two, v_vals, slope_one, dhidden, terms,
     own, first_cols, last_cols, west, east, row_in, halo_send_sem, halo_recv_sem, *scratch
 ):
     rows, cols, channels = fields.shape
     flat = (rows * cols, channels)
     halo = (own, first_cols, last_cols, west, east, row_in, halo_send_sem, halo_recv_sem)
     here = coordinates()
-    chain_one = Chain(0, here, terms, grad_one, scale, scratch)
-    chain_two = Chain(1, here, terms, grad_two, scale, scratch)
+    chain_one = Chain(0, here, terms, grad_one, scratch)
+    chain_two = Chain(1, here, terms, grad_two, scratch)
     barrier = pltpu.get_barrier_semaphore()
     awaited = greet_halo(barrier) + greet_reducers(here, barrier)
 
     halo_prepare(0, fields[...].astype(jnp.float32), halo)
-    extended[...] = jnp.zeros(extended.shape, extended.dtype)
-    fill_bands(taps_ahead, bands_ahead, cols)
     pl.semaphore_wait(barrier, awaited)
     halo_send(0, halo)
-    fill_bands(taps_back, bands_back, cols)
+    lat, lats = lax.axis_index("lat"), lax.axis_size("lat")
+    first = pl.multiple_of(lat * rows, rows)
+    at_top, at_bottom = lax.div(lats - 1 - lat, lats - 1), lax.div(lat, lats - 1)
+    extended[...] = jnp.zeros(extended.shape, extended.dtype)
+    load_taps(basis, taps, first, at_top, at_bottom)
+    fill_ahead(taps, widths, bands_ahead, first, cols)
+    fill_back(taps, widths, bands_back, first, lats * rows - 1, cols)
     halo_receive(0, halo, extended)
 
     apply_bands(bands_ahead, extended, u_one)
@@ -487,35 +551,18 @@
             copy.wait_send()
 
 
-def tap_lanes(taps):
-    kernels, rows, row_taps, lon_taps = taps.shape
-    lead = RIM + lon_taps // 2
-    period = 4 * RIM
-    spaced = jnp.pad(
-        taps.transpose(1, 0, 2, 3).astype(jnp.float32),
-        ((0, 0), (0, RING - kernels), (0, 0), (0, period - lon_taps)),
-    ).reshape(rows, RING, row_taps * period)
-    return jnp.pad(spaced, ((0, 0), (0, 0), (lead, LANES - lead - row_taps * period)))
-
-
 def body(fields, weight_one, weight_two, basis_raw, widths, cotangent):
     rows, cols, channels = fields.shape
     kernels = weight_one.shape[0]
-    basis = padded_basis(basis_raw, widths)
-    first_row = lax.axis_index("lat") * rows
-    ahead = lax.dynamic_slice_in_dim(basis, first_row + 2, rows, 1)
-    around = lax.dynamic_slice_in_dim(basis, first_row + 1, rows + 2, 1)
-    back = jnp.stack(
-        [around[:, side : side + rows, 2 - side, ::-1] for side in range(3)], axis=2
-    )
     scale = 1.0 / math.sqrt(rows * lax.axis_size("lat") * cols * lax.axis_size("lon"))
     grad_rows = kernels * channels // (2 * RING)
     low, high = jnp.bfloat16, jnp.float32
     height = (rows + 3) * (cols + 2 * RIM)
     stages = 4
     scratch = [
-        pltpu.VMEM((rows, RING * cols, LANES), low),
-        pltpu.VMEM((rows, RING * cols, LANES), low),
+        pltpu.VMEM((kernels, rows + 2, RING, LANES), high),
+        pltpu.VMEM((rows, kernels * cols, LANES), low),
+        pltpu.VMEM((rows, kernels * cols, LANES), low),
         pltpu.VMEM((height, channels), low),
         pltpu.VMEM((rows * cols, kernels * channels), low),
         pltpu.VMEM((rows * cols, kernels * channels), low),
@@ -534,20 +581,26 @@
     ] + reduce_scratch(grad_rows, channels)
     wide = jax.ShapeDtypeStruct((2, RING, grad_rows, channels), high)
     output, dfields, grad_one, grad_two = pl.pallas_call(
-        functools.partial(whole_kernel, scale),
+        whole_kernel,
         out_shape=(
-            jax.ShapeDtypeStruct(fields.shape, low),
-            jax.ShapeDtypeStruct(fields.shape, low),
+            jax.ShapeDtypeStruct(fields.shape, high),
+            jax.ShapeDtypeStruct(fields.shape, high),
             wide,
             wide,
         ),
-        in_specs=[pl.BlockSpec(memory_space=pltpu.VMEM)] * 6,
+        in_specs=[pl.BlockSpec(memory_space=pltpu.VMEM)] * 5
+        + [pl.BlockSpec(memory_space=pltpu.SMEM)],
         out_specs=(pl.BlockSpec(memory_space=pltpu.VMEM),) * 4,
         scratch_shapes=scratch,
         compiler_params=pltpu.CompilerParams(collective_id=0, has_side_effects=True),
-    )(fields, cotangent, weight_one, weight_two, tap_lanes(ahead), tap_lanes(back))
+    )(fields, cotangent, weight_one, weight_two, basis_raw, widths)
     shape = (kernels, channels, channels)
-    return output, dfields, grad_one.reshape(shape), grad_two.reshape(shape)
+    return (
+        output.astype(low),
+        dfields.astype(low),
+        grad_one.reshape(shape) * scale,
+        grad_two.reshape(shape) * scale,
+    )
 
 
 def solution(mesh):

time: 79.4 us -> 80.8 us (1.018)
  local copies, waits for them, and re-layouts: 6.27 us -> 1.87 us
  Pallas kernels: 70.4 us -> 73.7 us
  other arithmetic: 1.67 us -> 4.35 us
    unnamed x10 -> x3, local copies, waits for them, and re-layouts: 5.42 us -> 1.87 us
    pallas_call x1, Pallas kernels: 70.4 us -> 73.7 us  [body(): pl.pallas_call(whole_kernel, out_shape=(jax.ShapeDtypeStruct(fields.shape...]
    convert_element_type x2, other arithmetic: 0.09 us -> 2.22 us  [the longest x1 1.58 us: body(): output.astype(low)]
    mul x1, other arithmetic: 0.83 us -> 2.14 us  [body(): grad_two.reshape(shape) * scale]
where the time goes in v4:
time: 80.8 us; the launch traced here: 80.6 us
  Pallas kernels  73.7 us (91%)
  other arithmetic  4.35 us (5%)
  local copies, waits for them, and re-layouts  1.87 us (2%)
    pallas_call x1, Pallas kernels, body(): pl.pallas_call(whole_kernel, out_shape=(jax.ShapeDtypeStruct(fields.shape...  73.7 us
    mul x1, other arithmetic, body(): grad_two.reshape(shape) * scale  2.14 us
    unnamed x3, local copies, waits for them, and re-layouts  1.87 us

profile of v4, /device:TPU:1, one launch (start us, length us, event | category | flops | bytes accessed | tf_op | source)
XLA Modules:
  0.0 80.6 jit_solution(9924980672446534715)
XLA Ops:
  0.6 1.9 %copy.10.basis = bf16[7,64,3,9]{3,2,1,0:T(4,128)(2,1)} copy(bf16[7,64,3,9]{1,0,3,2:T(8,128)(2,1)} %param.9) | data formatting | bytes 48384 | tf_op args[3]
  2.5 73.7 %shard_map.93 = (f32[16,16,128]{2,1,0:T(8,128)}, f32[16,16,128]{2,1,0:T(8,128)}, f32[2,8,56,128]{3,2,1,0:T(8,128)}, f32[2,8,56,128]{3,2,1,0:T(8,128)}) custom-call(bf16[16,16,128]{2,1,0:T(8,128)(2,1)} %fields.1, bf16[16,16,128]{2,1,0:T(8,128)(2,1)} %cotangent.1, bf16[7,128,128]{2,1,0:T(8,128)(2,1)} %weight_one.1, bf16[7,128,128]{2,1,0:T(8,128)(2,1)} %weight_two.1, ...), custom_call_target="tpu_custom_call" | custom-call | tf_op jit(solution)/shard_map/pallas_call | solution.py:583
  76.2 0.0 copy-start
  76.2 1.6 %convert_element_type.6 = bf16[16,16,128]{2,1,0:T(8,128)(2,1)} convert(f32[16,16,128]{2,1,0:T(8,128)} %get-tuple-element.8) | non-fusion elementwise | flops 32768 | bytes 196608 | tf_op jit(solution)/shard_map/convert_element_type | solution.py:599
  77.8 0.0 copy-done
  77.8 0.6 convert_element_type.7
  78.4 2.1 %broadcast_multiply_fusion = (f32[2,8,56,128]{3,2,1,0:T(8,128)}, f32[2,8,56,128]{3,2,1,0:T(8,128)}) fusion(f32[2,8,56,128]{3,2,1,0:T(8,128)} %get-tuple-element.11, f32[2,8,56,128]{3,2,1,0:T(8,128)} %get-tuple-element.10), kind=kLoop, calls=%fused_computation | loop fusion | flops 229376 | bytes 1835008 | tf_op jit(solution)/shard_map/mul | solution.py:602
Async XLA Ops:
  76.2 1.6 %copy-start = (f32[16,16,128]{2,1,0:T(8,128)S(1)}, f32[16,16,128]{2,1,0:T(8,128)}, u32[]{:S(2)}) copy-start(f32[16,16,128]{2,1,0:T(8,128)} %get-tuple-element.9) | copy-start | bytes 393220

commit v5 on v3

--- a/solution.py
+++ b/solution.py
@@ -1,4 +1,3 @@
-import functools
 import math
 
 import jax
@@ -12,20 +11,10 @@
 RING = 8
 RIM = 8
 LANES = 128
+PERIOD = 4 * RIM
+LEAD = RIM + RIM // 2
 GELU_SLOPE = math.sqrt(2.0 / math.pi)
 GELU_CUBIC = 0.044715
-
-
-def padded_basis(basis_raw, widths):
-    tap_count = basis_raw.shape[3]
-    reach = (tap_count - 1) // 2
-    distance = jnp.abs(jnp.arange(tap_count, dtype=jnp.int32) - reach)
-    inside = (distance[None, :] <= widths[:, None]).astype(jnp.bfloat16)
-    masked = basis_raw * inside[None, :, None, :]
-    top_rows = masked[:, 0:1, ::-1, :]
-    bottom = masked[:, -1:, ::-1, :]
-    zero_row = jnp.zeros_like(top_rows)
-    return jnp.concatenate([zero_row, top_rows, masked, bottom, zero_row], axis=1)
 
 
 def coordinates():
@@ -84,13 +73,13 @@
 
 
 class Chain:
-    def __init__(self, which, here, terms, result, scale, scratch):
+    def __init__(self, which, here, terms, result, scratch):
         (self.pair_out, self.pair_in, self.halves, self.wide_out, self.wide_in, self.middle,
          self.last, self.chunk, self.other_half) = (ref.at[which] for ref in scratch[:9])
         self.pair_send, self.pair_recv, self.sends, self.recvs = (
             ref.at[which] for ref in scratch[9:]
         )
-        self.here, self.terms, self.result, self.scale = here, terms.at[which], result, scale
+        self.here, self.terms, self.result = here, terms.at[which], result
         self.core = here[0]
         self.at = [ring_index(here, axis) for axis in range(3)]
 
@@ -165,7 +154,7 @@
     def sum_third(self):
         for step in NEAR_FIRST:
             self.last_copy(step).wait_recv()
-        self.chunk[0] = (self.in_order(self.last, 2) * self.scale).astype(jnp.bfloat16)
+        self.chunk[0] = self.in_order(self.last, 2).astype(jnp.bfloat16)
         for step in FAR_FIRST:
             self.chunk_copy(step).start()
         self.across(0).start()
@@ -353,7 +342,7 @@
 
 
 def apply_bands(bands, extended, spread):
-    rows, height = bands.shape[0], bands.shape[1]
+    rows = bands.shape[0]
     kernels = spread.shape[1] // LANES
     cols = spread.shape[0] // rows
     period = cols + 2 * RIM
@@ -376,16 +365,49 @@
     lax.fori_loop(0, rows // group, some_rows, 0)
 
 
-def fill_bands(taps, bands, cols):
-    rows, kernels = taps.shape[0], taps.shape[1]
-
+def slant(lined, cols):
+    kernels = lined.shape[0]
+    level = jnp.broadcast_to(lined[:, None, :], (kernels, cols, LANES))
+    return pltpu.roll(level, 0, 2, stride=1, stride_axis=1).reshape(kernels * cols, LANES)
+
+
+def shifted_lane(shape):
+    return lax.broadcasted_iota(jnp.int32, shape, 1) + (PERIOD - LEAD)
+
+
+def within(lane, width):
+    return jnp.abs((lane & (PERIOD - 1)) - RIM // 2) <= width
+
+
+def fill_ahead(table, widths, bands, first, cols):
     def one_row(row, carry):
-        level = jnp.broadcast_to(taps[row][:, None, :], (kernels, cols, LANES))
-        slanted = pltpu.roll(level, 0, 2, stride=1, stride_axis=1)
-        bands[row] = slanted.reshape(kernels * cols, LANES).astype(bands.dtype)
+        seen = table[first + row][:, :LANES]
+        seen = jnp.where(within(shifted_lane(seen.shape), widths[first + row]), seen, 0.0)
+        bands[row] = slant(seen, cols).astype(bands.dtype)
         return carry
 
-    lax.fori_loop(0, rows, one_row, 0)
+    lax.fori_loop(0, bands.shape[0], one_row, 0)
+
+
+def fill_back(table, widths, bands, first, cols):
+    last_row = table.shape[0] - 1
+
+    def one_row(row, carry):
+        total = None
+        for side in range(3):
+            at = jnp.minimum(jnp.maximum(first + row + side - 1, 0), last_row)
+            seen = table[at][:, LANES:]
+            if side != 1:
+                end = 0 if side == 0 else last_row
+                seen = jnp.where(first + row == end, pltpu.roll(seen, LANES // 2, 1), seen)
+            lane = shifted_lane(seen.shape)
+            wanted = within(lane, widths[at]) & (lane // PERIOD == side + 1)
+            seen = jnp.where(wanted, seen, 0.0)
+            total = seen if total is None else total + seen
+        bands[row] = slant(total, cols).astype(bands.dtype)
+        return carry
+
+    lax.fori_loop(0, bands.shape[0], one_row, 0)
 
 
 def mixed_back(spread, weight):
@@ -402,7 +424,7 @@
 
 
 def whole_kernel(
-    scale, fields, cotangent, weight_one, weight_two, taps_ahead, taps_back,
+    fields, cotangent, weight_one, weight_two, table, widths,
     output, dfields, grad_one, grad_two,
     bands_ahead, bands_back, extended, u_one, u_two, v_vals, slope_one, dhidden, terms,
     own, first_cols, last_cols, west, east, row_in, halo_send_sem, halo_recv_sem, *scratch
@@ -411,17 +433,18 @@
     flat = (rows * cols, channels)
     halo = (own, first_cols, last_cols, west, east, row_in, halo_send_sem, halo_recv_sem)
     here = coordinates()
-    chain_one = Chain(0, here, terms, grad_one, scale, scratch)
-    chain_two = Chain(1, here, terms, grad_two, scale, scratch)
+    chain_one = Chain(0, here, terms, grad_one, scratch)
+    chain_two = Chain(1, here, terms, grad_two, scratch)
     barrier = pltpu.get_barrier_semaphore()
     awaited = greet_halo(barrier) + greet_reducers(here, barrier)
 
     halo_prepare(0, fields[...].astype(jnp.float32), halo)
     extended[...] = jnp.zeros(extended.shape, extended.dtype)
-    fill_bands(taps_ahead, bands_ahead, cols)
+    first = lax.axis_index("lat") * rows
+    fill_ahead(table, widths, bands_ahead, first, cols)
     pl.semaphore_wait(barrier, awaited)
     halo_send(0, halo)
-    fill_bands(taps_back, bands_back, cols)
+    fill_back(table, widths, bands_back, first, cols)
     halo_receive(0, halo, extended)
 
     apply_bands(bands_ahead, extended, u_one)
@@ -487,35 +510,27 @@
             copy.wait_send()
 
 
-def tap_lanes(taps):
-    kernels, rows, row_taps, lon_taps = taps.shape
-    lead = RIM + lon_taps // 2
-    period = 4 * RIM
-    spaced = jnp.pad(
-        taps.transpose(1, 0, 2, 3).astype(jnp.float32),
-        ((0, 0), (0, RING - kernels), (0, 0), (0, period - lon_taps)),
-    ).reshape(rows, RING, row_taps * period)
-    return jnp.pad(spaced, ((0, 0), (0, 0), (lead, LANES - lead - row_taps * period)))
+def tap_table(basis_raw):
+    _, _, row_taps, lon_taps = basis_raw.shape
+    shape = (row_taps, lon_taps, 2 * LANES)
+    row_tap, lon_tap, lane = (lax.broadcasted_iota(jnp.int32, shape, dim) for dim in range(3))
+    ahead = LEAD + PERIOD * row_tap + lon_tap
+    back = LANES + LEAD + PERIOD * (row_taps - 1 - row_tap) + lon_taps - 1 - lon_tap
+    placed = ((lane == ahead) | (lane == back)).astype(basis_raw.dtype)
+    return jnp.einsum("kirt,rtp->ikp", basis_raw, placed, preferred_element_type=jnp.float32)
 
 
 def body(fields, weight_one, weight_two, basis_raw, widths, cotangent):
     rows, cols, channels = fields.shape
     kernels = weight_one.shape[0]
-    basis = padded_basis(basis_raw, widths)
-    first_row = lax.axis_index("lat") * rows
-    ahead = lax.dynamic_slice_in_dim(basis, first_row + 2, rows, 1)
-    around = lax.dynamic_slice_in_dim(basis, first_row + 1, rows + 2, 1)
-    back = jnp.stack(
-        [around[:, side : side + rows, 2 - side, ::-1] for side in range(3)], axis=2
-    )
     scale = 1.0 / math.sqrt(rows * lax.axis_size("lat") * cols * lax.axis_size("lon"))
     grad_rows = kernels * channels // (2 * RING)
     low, high = jnp.bfloat16, jnp.float32
     height = (rows + 3) * (cols + 2 * RIM)
     stages = 4
     scratch = [
-        pltpu.VMEM((rows, RING * cols, LANES), low),
-        pltpu.VMEM((rows, RING * cols, LANES), low),
+        pltpu.VMEM((rows, kernels * cols, LANES), low),
+        pltpu.VMEM((rows, kernels * cols, LANES), low),
         pltpu.VMEM((height, channels), low),
         pltpu.VMEM((rows * cols, kernels * channels), low),
         pltpu.VMEM((rows * cols, kernels * channels), low),
@@ -534,20 +549,21 @@
     ] + reduce_scratch(grad_rows, channels)
     wide = jax.ShapeDtypeStruct((2, RING, grad_rows, channels), high)
     output, dfields, grad_one, grad_two = pl.pallas_call(
-        functools.partial(whole_kernel, scale),
+        whole_kernel,
         out_shape=(
             jax.ShapeDtypeStruct(fields.shape, low),
             jax.ShapeDtypeStruct(fields.shape, low),
             wide,
             wide,
         ),
-        in_specs=[pl.BlockSpec(memory_space=pltpu.VMEM)] * 6,
+        in_specs=[pl.BlockSpec(memory_space=pltpu.VMEM)] * 5
+        + [pl.BlockSpec(memory_space=pltpu.SMEM)],
         out_specs=(pl.BlockSpec(memory_space=pltpu.VMEM),) * 4,
         scratch_shapes=scratch,
         compiler_params=pltpu.CompilerParams(collective_id=0, has_side_effects=True),
-    )(fields, cotangent, weight_one, weight_two, tap_lanes(ahead), tap_lanes(back))
+    )(fields, cotangent, weight_one, weight_two, tap_table(basis_raw), widths)
     shape = (kernels, channels, channels)
-    return output, dfields, grad_one.reshape(shape), grad_two.reshape(shape)
+    return output, dfields, grad_one.reshape(shape) * scale, grad_two.reshape(shape) * scale
 
 
 def solution(mesh):

time: 79.4 us -> 78.4 us (0.987)
  local copies, waits for them, and re-layouts: 6.27 us -> 3.4 us
  other arithmetic: 1.67 us -> 2.67 us
    unnamed x10, local copies, waits for them, and re-layouts: 5.42 us -> 2.34 us
    mul x1 -> x2, other arithmetic: 0.83 us -> 2.67 us  [the longest x1 1.87 us: body(): grad_one.reshape(shape) * scale]
    dot_general x0 -> x1, local copies, waits for them, and re-layouts: none -> 1.06 us  [tap_table(): jnp.einsum('kirt,rtp->ikp', basis_raw, placed, preferred_element_type=jnp...]
where the time goes in v5:
time: 78.4 us; the launch traced here: 78 us
  Pallas kernels  71 us (91%)
  local copies, waits for them, and re-layouts  3.4 us (4%)
  other arithmetic  2.67 us (3%)
    pallas_call x1, Pallas kernels, body(): pl.pallas_call(whole_kernel, out_shape=(jax.ShapeDtypeStruct(fields.shape...  71 us
    unnamed x10, local copies, waits for them, and re-layouts  2.34 us
    mul x1, other arithmetic, body(): grad_one.reshape(shape) * scale  1.87 us

profile of v5, /device:TPU:1, one launch (start us, length us, event | category | flops | bytes accessed | tf_op | source)
XLA Modules:
  0.0 78.0 jit_solution(11270488437813868097)
XLA Ops:
  0.6 0.0 copy-start
  0.7 0.8 %copy-done = bf16[7,64,3,9]{1,0,3,2:T(8,128)(2,1)S(1)} copy-done((bf16[7,64,3,9]{1,0,3,2:T(8,128)(2,1)S(1)}, bf16[7,64,3,9]{1,0,3,2:T(8,128)(2,1)}, u32[]{:S(2)}) %copy-start) | copy-done | bytes 24216
  1.5 0.3 convolution_bitcast_fusion
  1.7 1.1 %copy.16 = f32[256,7,64]{0,1,2:T(8,128)} copy(f32[256,7,64]{0,2,1:T(8,128)S(1)} %convolution_bitcast_fusion) | data formatting | bytes 917504 | tf_op jit(solution)/shard_map/kirt,rtp->ikp/dot_general | solution.py:520
  2.8 71.0 %shard_map.93 = (bf16[16,16,128]{2,1,0:T(8,128)(2,1)}, bf16[16,16,128]{2,1,0:T(8,128)(2,1)}, f32[2,8,56,128]{3,2,1,0:T(8,128)}, f32[2,8,56,128]{3,2,1,0:T(8,128)}) custom-call(bf16[16,16,128]{2,1,0:T(8,128)(2,1)} %fields.1, bf16[16,16,128]{2,1,0:T(8,128)(2,1)} %cotangent.1, bf16[7,128,128]{2,1,0:T(8,128)(2,1)} %weight_one.1, ...), custom_call_target="tpu_custom_call" | custom-call | tf_op jit(solution)/shard_map/pallas_call | solution.py:551
  73.8 0.0 copy-start.1
  73.8 1.9 %broadcast_multiply_fusion.1 = f32[2,8,56,128]{3,2,1,0:T(8,128)} fusion(f32[2,8,56,128]{3,2,1,0:T(8,128)} %get-tuple-element.10), kind=kLoop, calls=%fused_computation.3 | loop fusion | flops 114688 | bytes 917504 | tf_op jit(solution)/shard_map/mul | solution.py:566
  75.7 0.0 copy-done.1
  75.7 0.0 copy-start.3
  75.7 0.8 %broadcast_multiply_fusion = f32[2,8,56,128]{3,2,1,0:T(8,128)} fusion(f32[2,8,56,128]{3,2,1,0:T(8,128)S(1)} %copy-done.1), kind=kLoop, calls=%fused_computation.2 | loop fusion | flops 114688 | bytes 917504 | tf_op jit(solution)/shard_map/mul | solution.py:566
  76.5 0.0 copy-done.3
  76.5 0.0 copy-start.2
  76.5 0.6 copy.19
  77.2 0.2 copy-done.2
  77.4 0.6 copy.20
  (1 shorter events, 0.0 us)
Async XLA Ops:
  0.6 0.8 %copy-start = (bf16[7,64,3,9]{1,0,3,2:T(8,128)(2,1)S(1)}, bf16[7,64,3,9]{1,0,3,2:T(8,128)(2,1)}, u32[]{:S(2)}) copy-start(bf16[7,64,3,9]{1,0,3,2:T(8,128)(2,1)} %param.9) | copy-start | bytes 72580
  73.8 1.9 %copy-start.1 = (f32[2,8,56,128]{3,2,1,0:T(8,128)S(1)}, f32[2,8,56,128]{3,2,1,0:T(8,128)}, u32[]{:S(2)}) copy-start(f32[2,8,56,128]{3,2,1,0:T(8,128)} %get-tuple-element.11) | copy-start | bytes 1376260
  75.7 0.8 %copy-start.3 = (bf16[16,16,128]{2,1,0:T(8,128)(2,1)S(1)}, bf16[16,16,128]{2,1,0:T(8,128)(2,1)}, u32[]{:S(2)}) copy-start(bf16[16,16,128]{2,1,0:T(8,128)(2,1)} %get-tuple-element.18) | copy-start | bytes 196612
  76.5 0.9 %copy-start.2 = (bf16[16,16,128]{2,1,0:T(8,128)(2,1)S(1)}, bf16[16,16,128]{2,1,0:T(8,128)(2,1)}, u32[]{:S(2)}) copy-start(bf16[16,16,128]{2,1,0:T(8,128)(2,1)} %get-tuple-element.19) | copy-start | bytes 196612
